TPU v7x, 128 devices: a whole 4x4x4 slice. The times are simulated.
128 devices in a mesh: dp: 16 (over z, x), tensor: 8 (over y, core).
Axes of the slice: x: 4, y: 4, z: 4, core: 2. Of those that a mesh axis runs over, the one named last changes fastest.
Arguments:
- tokens: bfloat16 [128, 128, 8192], P('dp', None, 'tensor'), may hold values from -6 to 6
- shared_prefix_tokens: bfloat16 [16, 256, 8192], P('dp', None, 'tensor'), may hold values from -6 to 6
- input_norm_gain: bfloat16 [8192], replicated, may hold values from 0.5 to 8
- query_weight: bfloat16 [8192, 8192], P(None, 'tensor'), may hold values from -0.0625 to 0.0625
- key_weight: bfloat16 [8192, 1024], P(None, 'tensor'), may hold values from -0.0625 to 0.0625
- value_weight: bfloat16 [8192, 1024], P(None, 'tensor'), may hold values from -0.0625 to 0.0625
- adapter_down_weight: bfloat16 [64, 8192, 16], P('dp', 'tensor'), may hold values from -0.0625 to 0.0625
- adapter_up_weight: bfloat16 [64, 16, 8192], P('dp', None, 'tensor'), may hold values from -0.75 to 0.75
- adapter_position: int32 [64], replicated, may hold values from 0 to 63, as said below
- request_adapter: int32 [128], P('dp'), may hold values from 0 to 63, as said below
- request_group: int32 [128], P('dp'), may hold values from 0 to 15
- lengths: int32 [128], P('dp'), may hold values from 1 to 128
- request_page_table: int32 [128, 1], P('dp'), may hold values from 0 to 127, as said below
Outputs:
- context: bfloat16 [128, 128, 8192], P('dp', None, 'tensor')
- paged_key_values: bfloat16 [128, 2, 128, 1024], P('dp', None, None, 'tensor')
Inputs may be any that keep to these rules, and one draw needn't show every extreme that they name: A permutation: adapter a is held at slot adapter_position[a], on index adapter_position[a] // 4 of dp. `request_adapter`: the 8 requests of one index of dp use adapters held by 8 different indices of dp. `request_page_table`: the requests of index i of dp use the pages i * 8 to (i + 1) * 8 - 1, each page once.
All inputs are finite; a program needn't handle non-finite values.
Results may differ from a plain program's by a relative error of at most 0.011.
The roundings to bfloat16 on the way count: a program that leaves them out, or rounds other values in their place, can miss the bound.
Values may be sent and summed in bfloat16 or wider, within the bound.
No kernel may reach another device: no remote copies, remote signals or barrier semaphores. Data moves between devices by JAX's collectives and lax.ppermute only.
A program may use at most 128 MiB of HBM per device.

v0:
```python
import functools

import jax
import jax.numpy as jnp
import numpy as np
from jax import lax
from jax.experimental import pallas as pl
from jax.experimental.pallas import tpu as pltpu
from jax.sharding import PartitionSpec as P

HEAD_WIDTH = 128
RANK = 16
EPS = 1e-05
THETA = 500000.0
ADAPTER_SCALE = 2.0
F32 = jnp.float32
BF16 = jnp.bfloat16
CHUNKS = (4, 4)
BLOCKS = ((0, 0, 2), (0, 2, 2), (1, 0, 4))

SWAP = [(y * 2 + c, y * 2 + 1 - c) for y in range(4) for c in range(2)]
RING = [(y * 2 + c, (y + 1 - 2 * c) % 4 * 2 + c) for y in range(4) for c in range(2)]
BACK = [(y * 2 + c, (y - 1 + 2 * c) % 4 * 2 + c) for y in range(4) for c in range(2)]


def plane_shift(k, stage):
    pairs = []
    for z in range(4):
        for x in range(4):
            for t in range(8):
                along_x = (t % 2 == 0) == (stage == 0)
                to_z, to_x = (z, (x + k) % 4) if along_x else ((z + k) % 4, x)
                pairs.append(((z * 4 + x) * 8 + t, (to_z * 4 + to_x) * 8 + t))
    return pairs


def over_tensor(value, pairs):
    return lax.ppermute(value, "tensor", pairs)


def over_plane(value, stage):
    send = lambda k: lax.ppermute(value, ("dp", "tensor"), plane_shift(k, stage))
    return [value, send(-1), send(2), send(1)]


def gather_plane(value):
    first = jnp.stack(over_plane(value, 0))
    return over_plane(first, 1)


def rotate_tables(start, count):
    half = HEAD_WIDTH // 2
    freq = THETA ** (-(np.arange(half) * 2.0 / HEAD_WIDTH))
    angle = np.arange(start, start + count)[:, None] * freq[None, :]
    cosine, sine = np.cos(angle), np.sin(angle)
    return (
        np.concatenate([cosine, cosine], 1).astype(np.float32),
        np.concatenate([-sine, sine], 1).astype(np.float32),
    )


def rotate(value, cosine, sine):
    return value * cosine + pltpu.roll(value, HEAD_WIDTH // 2, 1) * sine


def dot(a, b, dims=((1,), (0,))):
    return lax.dot_general(a, b, (dims, ((), ())), preferred_element_type=F32)


def norm_kernel(place, own, other, scale, gain_own, gain_other, out):
    for r in range(own.shape[0]):
        row = jnp.broadcast_to(scale[r], (128, 128))
        eye = lax.broadcasted_iota(jnp.int32, (128, 128), 0) == lax.broadcasted_iota(
            jnp.int32, (128, 128), 1
        )
        column = jnp.sum(jnp.where(eye, row, 0.0), axis=1, keepdims=True)
        out[0, r] = (own[r].astype(F32) * column * gain_own[0]).astype(BF16)
        out[1, r] = (other[r].astype(F32) * column * gain_other[0]).astype(BF16)


def norm_call(first, count, gain_ids, own, other, scale, gain):
    _, seq, part = own.shape
    rows = lambda i, ids: (first + i, 0, 0)
    return pl.pallas_call(
        norm_kernel,
        out_shape=jax.ShapeDtypeStruct((2, count, seq, part), BF16),
        grid_spec=pltpu.PrefetchScalarGridSpec(
            num_scalar_prefetch=1,
            grid=(count,),
            in_specs=[
                pl.BlockSpec((1, seq, part), rows),
                pl.BlockSpec((1, seq, part), rows),
                pl.BlockSpec((1, 1, seq), rows),
                pl.BlockSpec((1, 1, part), lambda i, ids: (ids[0], 0, 0)),
                pl.BlockSpec((1, 1, part), lambda i, ids: (ids[1], 0, 0)),
            ],
            out_specs=pl.BlockSpec((2, 1, seq, part), lambda i, ids: (0, i, 0, 0)),
        ),
        name="norm",
    )(gain_ids, own, other, scale, gain, gain)


def prefix_kernel(order, mine, near, cross, far, far_cross, gain, kw, vw, cosine, sine, out):
    width = mine.shape[-1]
    pieces = [mine[0], mine[1], near[0], near[1], cross[0], cross[1], far[...], far_cross[...]]
    total = jnp.zeros((mine.shape[1], 1), F32)
    for piece in pieces:
        value = piece.astype(F32)
        total = total + jnp.sum(value * value, axis=1, keepdims=True)
    scale = lax.rsqrt(total * (1.0 / (8 * width)) + EPS)
    acc = jnp.zeros((mine.shape[1], 2 * HEAD_WIDTH), F32)
    for i, piece in enumerate(pieces):
        block = order[i]
        at = pl.ds(pl.multiple_of(block * width, width), width)
        weight = jnp.concatenate([kw[at, :], vw[at, :]], axis=1)
        normed = (piece.astype(F32) * scale * gain[block]).astype(BF16)
        acc = acc + dot(normed, weight)
    out[0] = rotate(acc[:, :HEAD_WIDTH], cosine[...], sine[...]).astype(BF16)
    out[1] = acc[:, HEAD_WIDTH:].astype(BF16)


def prefix_call(order, mine, near, cross, far, far_cross, gain, kw, vw, cosine, sine):
    rows = mine.shape[1]
    full = pl.BlockSpec(memory_space=pltpu.VMEM)
    return pl.pallas_call(
        prefix_kernel,
        out_shape=jax.ShapeDtypeStruct((2, rows, HEAD_WIDTH), BF16),
        in_specs=[pl.BlockSpec(memory_space=pltpu.SMEM)] + [full] * 10,
        out_specs=full,
        name="prefix",
    )(order, mine, near, cross, far, far_cross, gain, kw, vw, cosine, sine)


def pick_copies(sources, select, first, second, target, sem, act):
    for j, source in enumerate(sources):

        @pl.when(select == j)
        def _(source=source):
            act(pltpu.make_async_copy(source.at[first] if second is None else source.at[first, second], target, sem))


def low_kernel(pick, x0, x1, a0, a1, a2, a3, part, up, held, sems):
    for r in range(held.shape[0]):
        pick_copies(
            (a0, a1, a2, a3), pick[r, 0], pick[r, 1], pick[r, 2], held.at[r], sems.at[r], lambda c: c.start()
        )
    r = 0
    for x in (x0, x1):
        for i in range(x.shape[1]):
            pltpu.make_async_copy(a0.at[0, 0], held.at[r], sems.at[r]).wait()
            part[r] = dot(held[r, :RANK], x[0, i], ((1,), (1,)))
            up[r] = held[r, RANK:]
            r += 1


def low_call(pick, chunks, adapters):
    requests = pick.shape[0]
    seq, part = chunks[0].shape[2:]
    full = pl.BlockSpec(memory_space=pltpu.VMEM)
    some = [pl.BlockSpec((1,) + c.shape[1:], lambda i, *_: (0, 0, 0, 0)) for c in chunks]
    return pl.pallas_call(
        low_kernel,
        out_shape=(
            jax.ShapeDtypeStruct((requests, RANK, seq), F32),
            jax.ShapeDtypeStruct((requests, RANK, part), BF16),
        ),
        grid_spec=pltpu.PrefetchScalarGridSpec(
            num_scalar_prefetch=1,
            grid=(1,),
            in_specs=some + [pl.BlockSpec(memory_space=pl.ANY)] * 4,
            out_specs=[
                pl.BlockSpec((requests, RANK, seq), lambda i, *_: (0, 0, 0)),
                pl.BlockSpec((requests, RANK, part), lambda i, *_: (0, 0, 0)),
            ],
            scratch_shapes=[
                pltpu.VMEM((requests, 2 * RANK, part), BF16),
                pltpu.SemaphoreType.DMA((requests,)),
            ],
        ),
        name="low",
    )(pick, *chunks, *adapters)


def block_kernel(
    first,
    start,
    count,
    order,
    table,
    mine,
    near,
    cross,
    far,
    far_cross,
    qw,
    kw,
    vw,
    low,
    up,
    cosine,
    sine,
    p0,
    p1,
    p2,
    p3,
    *rest,
):
    context, pages, xs, acc_q, acc_kv, pairs, page, x_sem, pair_sem, page_sem = rest[-10:]
    k = pl.program_id(0)
    seq, width = xs.shape[2:]
    pre = pairs.shape[2]
    sources = [mine.at[0], mine.at[1], near.at[0], near.at[1], cross.at[0], cross.at[1], far, far_cross]

    @pl.when(k == 0)
    def _():
        for i, source in enumerate(sources):
            pltpu.make_async_copy(source.at[start : start + count], xs.at[i], x_sem.at[i]).start()
        for r in range(count):
            pick_copies(
                (p0, p1, p2, p3),
                table[first + r, 0],
                table[first + r, 1],
                None,
                pairs.at[r],
                pair_sem.at[r],
                lambda c: c.start(),
            )

    pltpu.make_async_copy(far.at[start : start + count], xs.at[k], x_sem.at[k]).wait()
    x = xs[k].reshape(count * seq, width)
    part_q = dot(x, qw[...])
    part_kv = dot(x, jnp.concatenate([kw[...], vw[...]], axis=1))

    @pl.when(k == 0)
    def _():
        acc_q[...] = part_q
        acc_kv[...] = part_kv

    @pl.when(k > 0)
    def _():
        acc_q[...] += part_q
        acc_kv[...] += part_kv

    @pl.when(k == pl.num_programs(0) - 1)
    def _():
        heads = acc_q.shape[1] // HEAD_WIDTH
        cos_t, sin_t = cosine[...], sine[...]
        token = lax.broadcasted_iota(jnp.int32, (seq, HEAD_WIDTH), 0)
        causal = lax.broadcasted_iota(jnp.int32, (seq, seq), 1) <= lax.broadcasted_iota(
            jnp.int32, (seq, seq), 0
        )
        allowed = jnp.concatenate([jnp.ones((seq, pre), jnp.bool_), causal], axis=1)

        def request(r, carry):
            pltpu.make_async_copy(p0.at[0], pairs.at[r], pair_sem.at[r]).wait()
            live = token < table[first + r, 2]
            rows = pl.ds(pl.multiple_of(r * seq, seq), seq)
            key = rotate(acc_kv[rows, :HEAD_WIDTH], cos_t, sin_t)
            key = jnp.where(live, key, 0.0).astype(BF16)
            value = jnp.where(live, acc_kv[rows, HEAD_WIDTH:], 0.0).astype(BF16)
            page[r, 0] = key
            page[r, 1] = value
            pltpu.make_async_copy(page.at[r], pages.at[table[first + r, 3]], page_sem.at[r]).start()
            keys = jnp.concatenate([pairs[r, 0], key], axis=0)
            values = jnp.concatenate([pairs[r, 1], value], axis=0)
            delta = ADAPTER_SCALE * dot(low[first + r], up[first + r], ((0,), (0,)))
            query = acc_q[rows, :] + delta.astype(BF16).astype(F32)
            for h in range(heads):
                lanes = slice(h * HEAD_WIDTH, (h + 1) * HEAD_WIDTH)
                q = rotate(query[:, lanes], cos_t, sin_t).astype(BF16)
                scores = dot(q, keys, ((1,), (1,))) * (HEAD_WIDTH**-0.5)
                scores = jnp.where(allowed, scores, -1e30)
                top = jnp.max(scores, axis=1, keepdims=True)
                weights = jnp.exp(scores - top)
                inverse = 1.0 / jnp.sum(weights, axis=1, keepdims=True)
                probs = (weights * inverse).astype(BF16)
                out = dot(probs, values)
                context[r, :, lanes] = jnp.where(live, out, 0.0).astype(BF16)
            return carry

        lax.fori_loop(0, count, request, 0)
        for r in range(count):
            pltpu.make_async_copy(page.at[r], pages.at[0], page_sem.at[r]).wait()


def block_call(first, start, count, requests, order, table, x, weights, low, up, tables, pairs, before):
    seq, width = x[0].shape[2:]
    q_width = weights[0].shape[1]
    pre = pairs[0].shape[2]
    hbm = pl.BlockSpec(memory_space=pl.ANY)
    whole = lambda a: pl.BlockSpec(a.shape, lambda k, *_: (0,) * a.ndim)
    weight = lambda a: pl.BlockSpec((width, a.shape[1]), lambda k, order, table: (order[k], 0))
    operands = [*x, *weights, low, up, *tables, *pairs, *before]
    specs = (
        [hbm] * 5
        + [weight(w) for w in weights]
        + [whole(low), whole(up)]
        + [whole(t) for t in tables]
        + [hbm] * (4 + len(before))
    )
    at = len(operands)
    aliases = {at: 0, at + 1: 1} if before else {}
    return pl.pallas_call(
        functools.partial(block_kernel, first, start, count),
        out_shape=(
            jax.ShapeDtypeStruct((requests, seq, q_width), BF16),
            jax.ShapeDtypeStruct((requests, 2, seq, HEAD_WIDTH), BF16),
        ),
        grid_spec=pltpu.PrefetchScalarGridSpec(
            num_scalar_prefetch=2,
            grid=(8,),
            in_specs=specs,
            out_specs=[pl.BlockSpec((count, seq, q_width), lambda k, *_: (first // count, 0, 0)), hbm],
            scratch_shapes=[
                pltpu.VMEM((8, count, seq, width), BF16),
                pltpu.VMEM((count * seq, q_width), F32),
                pltpu.VMEM((count * seq, 2 * HEAD_WIDTH), F32),
                pltpu.VMEM((count, 2, pre, HEAD_WIDTH), BF16),
                pltpu.VMEM((count, 2, seq, HEAD_WIDTH), BF16),
                pltpu.SemaphoreType.DMA((8,)),
                pltpu.SemaphoreType.DMA((count,)),
                pltpu.SemaphoreType.DMA((count,)),
            ],
        ),
        input_output_aliases=aliases,
        name="block",
    )(order, table, *operands)


def after(values, *others):
    return lax.optimization_barrier((tuple(values), others))[0]


def ring_rest(near):
    far = over_tensor(near[0], RING)
    return near, over_tensor(near, SWAP), far, over_tensor(far, SWAP)


def on_device(
    tokens,
    shared_prefix_tokens,
    input_norm_gain,
    query_weight,
    key_weight,
    value_weight,
    adapter_down_weight,
    adapter_up_weight,
    adapter_position,
    request_adapter,
    request_group,
    lengths,
    request_page_table,
):
    requests, seq, part = tokens.shape
    pre = shared_prefix_tokens.shape[1]
    held = adapter_up_weight.shape[0]
    column = lax.axis_index("tensor")
    place = lax.axis_index("dp")
    core = column % 2
    y = column // 2
    z_at, x_at = place // 4, place % 4

    near_y = (y + 3 + 2 * core) % 4
    cross_y = (y + 1 + 2 * core) % 4
    far_y = (y + 2) % 4
    order = jnp.stack(
        [
            column,
            column ^ 1,
            near_y * 2 + core,
            near_y * 2 + 1 - core,
            cross_y * 2 + 1 - core,
            cross_y * 2 + core,
            far_y * 2 + core,
            far_y * 2 + 1 - core,
        ]
    ).astype(jnp.int32)

    def relative(owner):
        dz, dx = (owner // 4 - z_at) % 4, (owner % 4 - x_at) % 4
        return jnp.where(core == 0, dx, dz), jnp.where(core == 0, dz, dx)

    prefix = shared_prefix_tokens.reshape(pre, part)
    prefix_other = over_tensor(prefix, SWAP)
    tokens_other = over_tensor(tokens, SWAP)
    prefix_mine = jnp.stack([prefix, prefix_other])
    prefix_near = over_tensor(prefix_mine, RING)

    square = lambda v: jnp.sum(jnp.square(v.astype(F32)), axis=-1)
    chip = square(tokens) + square(tokens_other)
    one = over_tensor(chip, BACK)
    two = over_tensor(one, BACK)
    mean = (chip + two + one + over_tensor(one, SWAP)) * (1.0 / (8 * part))
    scale = lax.rsqrt(mean + EPS).reshape(requests, 1, seq)

    prefix_rest = ring_rest(after((prefix_near,), scale)[0])
    down, up = after((adapter_down_weight, adapter_up_weight), scale)
    adapters = gather_plane(jnp.concatenate([down.transpose(0, 2, 1), up], axis=1))

    gain = input_norm_gain.astype(F32).reshape(8, 1, part)
    firsts = [sum(CHUNKS[:i]) for i in range(len(CHUNKS))]
    chunks = [
        norm_call(f, n, order[:2], tokens, tokens_other, scale, gain)
        for f, n in zip(firsts, CHUNKS)
    ]
    near = over_tensor(after(chunks[:1], prefix_rest[2])[0], RING)
    pre_cos, pre_sin = rotate_tables(0, pre)
    pair = prefix_call(
        order, prefix_mine, *prefix_rest, gain, key_weight, value_weight, pre_cos, pre_sin
    )
    pair_row = jnp.stack(over_plane(pair, 0))
    pairs = over_plane(pair_row, 1)

    ids = jnp.arange(adapter_position.shape[0])
    slots = jnp.sum(
        jnp.where(request_adapter[:, None] == ids[None, :], adapter_position[None, :], 0), axis=1
    )
    slot_1, slot_2 = relative(slots // held)
    pick = jnp.stack([slot_2, slot_1, slots % held], axis=1).astype(jnp.int32)
    part_low, up = low_call(pick, chunks, adapters)
    near = after((near,), part_low, pair_row)[0]
    chip_low = part_low + over_tensor(part_low, SWAP)
    one_low = over_tensor(chip_low, BACK)
    two_low = over_tensor(one_low, BACK)
    low = (chip_low + two_low + one_low + over_tensor(one_low, SWAP)).astype(BF16)
    far = after((over_tensor(near[0], RING),), low, *pairs)[0]
    gathered = [chunks[0], near, over_tensor(near, SWAP), far, over_tensor(far, SWAP)]
    late_near = over_tensor(after(chunks[1:], far)[0], RING)

    group_1, group_2 = relative(request_group)
    page = request_page_table.reshape(-1) - place * requests
    table = jnp.stack([group_2, group_1, lengths, page], axis=1).astype(jnp.int32)
    tables = rotate_tables(pre, seq)
    outs = ()
    for i, (chunk, start, count) in enumerate(BLOCKS):
        if i == 1:
            late_near, outs = lax.optimization_barrier((late_near, outs))
            late_far = over_tensor(late_near[0], RING)
            late_cross = over_tensor(late_near, SWAP)
        if i == 2:
            late_far, outs = lax.optimization_barrier((late_far, outs))
            late_far_cross = over_tensor(late_far, SWAP)
            gathered = [chunks[1], late_near, late_cross, late_far, late_far_cross]
        outs = block_call(
            firsts[chunk] + start,
            start,
            count,
            requests,
            order,
            table,
            gathered,
            (query_weight, key_weight, value_weight),
            low,
            up,
            tables,
            pairs,
            outs,
        )
    return outs


def solution(mesh):
    in_specs = (
        P("dp", None, "tensor"),
        P("dp", None, "tensor"),
        P(),
        P(None, "tensor"),
        P(None, "tensor"),
        P(None, "tensor"),
        P("dp", "tensor", None),
        P("dp", None, "tensor"),
        P(),
        P("dp"),
        P("dp"),
        P("dp"),
        P("dp", None),
    )
    out_specs = (P("dp", None, "tensor"), P("dp", None, None, "tensor"))
    return jax.shard_map(
        on_device, mesh=mesh, in_specs=in_specs, out_specs=out_specs, check_vma=False
    )
```

profile of v0, /device:TPU:1, one launch (start us, length us, event | category | flops | bytes accessed | tf_op | source)
XLA Modules:
  0.0 202.7 jit_solution(18094944834149381430)
XLA Ops:
  0.6 1.5 collective-permute-start
  2.2 4.7 %collective-permute-done.4 = bf16[256,1024]{1,0:T(8,128)(2,1)S(1)} collective-permute-done((bf16[256,1024]{1,0:T(8,128)(2,1)}, bf16[256,1024]{1,0:T(8,128)(2,1)S(1)}, u32[]{:S(2)}, u32[]{:S(2)}) %collective-permute-start.4) | collective-permute-done | bytes 524320 | tf_op jit(solution)/shard_map/ppermute | solution.py:38
  6.9 1.1 pad_maximum_fusion.mine
  8.0 2.9 %collective-permute-start.5 = (bf16[2,256,1024]{2,1,0:T(8,128)(2,1)S(1)}, bf16[2,256,1024]{2,1,0:T(8,128)(2,1)S(1)}, u32[]{:S(2)}, u32[]{:S(2)}) collective-permute-start(bf16[2,256,1024]{2,1,0:T(8,128)(2,1)S(1)} %pad_maximum_fusion.mine), channel_id=1, source_target_pairs={{0,2},{1,7},{2,4},{3,1},{4,6},{5,3},{6,0},{7,5},{8,10},{9,15},{10,... | collective-permute-start | bytes 3145736 | tf_op jit(solution)/shard_map/ppermute | solution.py:38
  11.4 1.3 copy-done.1
  13.3 4.1 %collective-permute-done.1 = f32[8,128]{1,0:T(8,128)S(1)} collective-permute-done((f32[8,128]{1,0:T(8,128)S(1)}, f32[8,128]{1,0:T(8,128)S(1)}, u32[]{:S(2)}, u32[]{:S(2)}) %collective-permute-start.1) | collective-permute-done | bytes 4128 | tf_op jit(solution)/shard_map/ppermute | solution.py:38
  17.6 1.0 collective-permute-done.3
  18.6 2.9 %collective-permute-done.2 = f32[8,128]{1,0:T(8,128)S(1)} collective-permute-done((f32[8,128]{1,0:T(8,128)S(1)}, f32[8,128]{1,0:T(8,128)S(1)}, u32[]{:S(2)}, u32[]{:S(2)}) %collective-permute-start.2) | collective-permute-done | bytes 4128 | tf_op jit(solution)/shard_map/ppermute | solution.py:38
  22.1 0.7 collective-permute-done.5.near
  22.8 3.2 %collective-permute-start.6 = (bf16[256,1024]{1,0:T(8,128)(2,1)S(1)}, bf16[256,1024]{1,0:T(8,128)(2,1)}, u32[]{:S(2)}, u32[]{:S(2)}) collective-permute-start(bf16[256,1024]{1,0:T(8,128)(2,1)S(1)} %slice_bitcast_fusion.2), channel_id=1, source_target_pairs={{0,2},{1,7},{2,4},{3,1},{4,6},{5,3},{6,0},{7,5},{8,10},{9,15},{10,... | collective-permute-start | bytes 1572872 | tf_op jit(solution)/shard_map/ppermute | solution.py:38
  27.2 4.9 %norm.3.x0.mine = bf16[2,4,128,1024]{3,2,1,0:T(8,128)(2,1)} custom-call(s32[2]{0:T(128)} %pad_add_fusion.2.place, bf16[8,128,1024]{2,1,0:T(8,128)(2,1)} %own.3, bf16[8,128,1024]{2,1,0:T(8,128)(2,1)} %copy-done.1, f32[8,1,128]{2,1,0:T(1,128)} %bitcast.49, f32[8,1,1024]{2,1,0:T(1,128)} %bitcast.34, f32[8,1,1024]{2,1,0:T(1,128)} %bitcast.35), custom_call_target="tpu_custom_call" | custom-call | tf_op jit(solution)/shard_map/norm/pallas_call | solution.py:84
  32.1 3.2 %collective-permute-start.7 = (bf16[2,4,128,1024]{3,2,1,0:T(8,128)(2,1)}, bf16[2,4,128,1024]{3,2,1,0:T(8,128)(2,1)}, u32[]{:S(2)}, u32[]{:S(2)}) collective-permute-start(bf16[2,4,128,1024]{3,2,1,0:T(8,128)(2,1)} %norm.3.x0.mine), channel_id=1, source_target_pairs={{0,2},{1,7},{2,4},{3,1},{4,6},{5,3},{6,0},{7,5},{8,10},{9,15},{10,... | collective-permute-start | bytes 6291464 | tf_op jit(solution)/shard_map/ppermute | solution.py:38
  35.4 3.7 %collective-permute-start.9 = (bf16[4,32,1024]{2,1,0:T(8,128)(2,1)S(1)}, bf16[4,32,1024]{2,1,0:T(8,128)(2,1)S(1)}, u32[]{:S(2)}, u32[]{:S(2)}) collective-permute-start(bf16[4,32,1024]{2,1,0:T(8,128)(2,1)S(1)} %get-tuple-element.44), channel_id=1, source_target_pairs={{0,16},{1,65},{2,18},{3,67},{4,20},{5,69},{6,22},{7,71},{8,24},{9,... | collective-permute-start | bytes 786440 | tf_op jit(solution)/shard_map/ppermute | solution.py:42
  39.5 1.0 collective-permute-start.10
  40.5 2.3 %collective-permute-done.9 = bf16[4,32,1024]{2,1,0:T(8,128)(2,1)S(1)} collective-permute-done((bf16[4,32,1024]{2,1,0:T(8,128)(2,1)S(1)}, bf16[4,32,1024]{2,1,0:T(8,128)(2,1)S(1)}, u32[]{:S(2)}, u32[]{:S(2)}) %collective-permute-start.9) | collective-permute-done | bytes 262176 | tf_op jit(solution)/shard_map/ppermute | solution.py:42
  43.2 3.6 %collective-permute-done.8 = bf16[4,32,1024]{2,1,0:T(8,128)(2,1)S(1)} collective-permute-done((bf16[4,32,1024]{2,1,0:T(8,128)(2,1)S(1)}, bf16[4,32,1024]{2,1,0:T(8,128)(2,1)S(1)}, u32[]{:S(2)}, u32[]{:S(2)}) %collective-permute-start.8) | collective-permute-done | bytes 262176 | tf_op jit(solution)/shard_map/ppermute | solution.py:42
  47.0 1.3 collective-permute-start.13
  48.2 2.5 %collective-permute-start.12 = (bf16[4,4,32,1024]{3,2,1,0:T(8,128)(2,1)S(1)}, bf16[4,4,32,1024]{3,2,1,0:T(8,128)(2,1)}, u32[]{:S(2)}, u32[]{:S(2)}) collective-permute-start(bf16[4,4,32,1024]{3,2,1,0:T(8,128)(2,1)S(1)} %pad_maximum_fusion.1.a0), channel_id=1, source_target_pairs={{0,64},{1,17},{2,66},{3,19},{4,68},{5,21},{6,70},{7,23},{8,72},{9,... | collective-permute-start | bytes 3145736 | tf_op jit(solution)/shard_map/ppermute | solution.py:42
  50.7 1.2 collective-permute-start.11
  52.4 6.4 %prefix.1 = bf16[2,256,128]{2,1,0:T(8,128)(2,1)} custom-call(s32[8]{0:T(128)} %stack.92.order, bf16[2,256,1024]{2,1,0:T(8,128)(2,1)} %copy-done.7, bf16[2,256,1024]{2,1,0:T(8,128)(2,1)} %copy-done.9, bf16[2,256,1024]{2,1,0:T(8,128)(2,1)} %copy-done.11, bf16[256,1024]{1,0:T(8,128)(2,1)} %collective-permute-done.6.far, ...), custom_call_target="tpu_custom_call" | custom-call | tf_op jit(solution)/shard_map/prefix/pallas_call | solution.py:125
  58.8 0.7 collective-permute-start.18
  59.5 5.4 %collective-permute-done.18 = bf16[2,256,128]{2,1,0:T(8,128)(2,1)S(1)} collective-permute-done((bf16[2,256,128]{2,1,0:T(8,128)(2,1)}, bf16[2,256,128]{2,1,0:T(8,128)(2,1)S(1)}, u32[]{:S(2)}, u32[]{:S(2)}) %collective-permute-start.18) | collective-permute-done | bytes 131104 | tf_op jit(solution)/shard_map/ppermute | solution.py:42
  64.9 13.2 %collective-permute-start.17 = (bf16[2,256,128]{2,1,0:T(8,128)(2,1)}, bf16[2,256,128]{2,1,0:T(8,128)(2,1)S(1)}, u32[]{:S(2)}, u32[]{:S(2)}) collective-permute-start(bf16[2,256,128]{2,1,0:T(8,128)(2,1)} %prefix.1), channel_id=1, source_target_pairs={{0,16},{1,65},{2,18},{3,67},{4,20},{5,69},{6,22},{7,71},{8,24},{9,... | collective-permute-start | bytes 393224 | tf_op jit(solution)/shard_map/ppermute | solution.py:42
  78.4 2.3 %collective-permute-done.17 = bf16[2,256,128]{2,1,0:T(8,128)(2,1)S(1)} collective-permute-done((bf16[2,256,128]{2,1,0:T(8,128)(2,1)}, bf16[2,256,128]{2,1,0:T(8,128)(2,1)S(1)}, u32[]{:S(2)}, u32[]{:S(2)}) %collective-permute-start.17) | collective-permute-done | bytes 131104 | tf_op jit(solution)/shard_map/ppermute | solution.py:42
  80.7 0.7 pad_add_fusion.1.pick
  81.4 4.9 %norm.2.x1.mine = bf16[2,4,128,1024]{3,2,1,0:T(8,128)(2,1)} custom-call(s32[2]{0:T(128)} %pad_add_fusion.2.place, bf16[8,128,1024]{2,1,0:T(8,128)(2,1)} %own.3, bf16[8,128,1024]{2,1,0:T(8,128)(2,1)} %copy-done.1, f32[8,1,128]{2,1,0:T(1,128)} %bitcast.50, f32[8,1,1024]{2,1,0:T(1,128)} %bitcast.37, f32[8,1,1024]{2,1,0:T(1,128)} %bitcast.38), custom_call_target="tpu_custom_call" | custom-call | tf_op jit(solution)/shard_map/norm/pallas_call | solution.py:84
  86.4 5.8 %low.1 = (f32[8,16,128]{2,1,0:T(8,128)}, bf16[8,16,1024]{2,1,0:T(8,128)(2,1)}) custom-call(s32[8,3]{1,0:T(8,128)} %pad_add_fusion.1.pick, bf16[2,4,128,1024]{3,2,1,0:T(8,128)(2,1)} %norm.3.x0.mine, bf16[2,4,128,1024]{3,2,1,0:T(8,128)(2,1)} %norm.2.x1.mine, bf16[4,4,32,1024]{3,2,1,0:T(8,128)(2,1)} %copy-done.8, ...), custom_call_target="tpu_custom_call" | custom-call | tf_op jit(solution)/shard_map/low/pallas_call | solution.py:161
  92.3 1.4 slice_bitcast_fusion.1
  94.3 2.5 %collective-permute-start.24 = (bf16[4,2,256,128]{3,2,1,0:T(8,128)(2,1)S(1)}, bf16[4,2,256,128]{3,2,1,0:T(8,128)(2,1)S(1)}, u32[]{:S(2)}, u32[]{:S(2)}) collective-permute-start(bf16[4,2,256,128]{3,2,1,0:T(8,128)(2,1)S(1)} %pad_maximum_fusion.2.p0), channel_id=1, source_target_pairs={{0,96},{1,25},{2,98},{3,27},{4,100},{5,29},{6,102},{7,31},{8,104},... | collective-permute-start | bytes 1572872 | tf_op jit(solution)/shard_map/ppermute | solution.py:42
  96.8 1.5 collective-permute-done.20
  98.2 0.9 add.205
  99.1 1.3 collective-permute-start.21
  100.3 4.3 %collective-permute-done.21 = f32[8,16,128]{2,1,0:T(8,128)S(1)} collective-permute-done((f32[8,16,128]{2,1,0:T(8,128)S(1)}, f32[8,16,128]{2,1,0:T(8,128)S(1)}, u32[]{:S(2)}, u32[]{:S(2)}) %collective-permute-start.21) | collective-permute-done | bytes 65568 | tf_op jit(solution)/shard_map/ppermute | solution.py:38
  104.6 1.3 collective-permute-done.23
  105.9 4.3 %collective-permute-done.22 = f32[8,16,128]{2,1,0:T(8,128)S(1)} collective-permute-done((f32[8,16,128]{2,1,0:T(8,128)S(1)}, f32[8,16,128]{2,1,0:T(8,128)S(1)}, u32[]{:S(2)}, u32[]{:S(2)}) %collective-permute-start.22) | collective-permute-done | bytes 65568 | tf_op jit(solution)/shard_map/ppermute | solution.py:38
  110.2 0.6 add_convert_fusion.low
  111.0 2.2 %collective-permute-start.27 = (bf16[2,4,128,1024]{3,2,1,0:T(8,128)(2,1)S(1)}, bf16[2,4,128,1024]{3,2,1,0:T(8,128)(2,1)}, u32[]{:S(2)}, u32[]{:S(2)}) collective-permute-start(bf16[2,4,128,1024]{3,2,1,0:T(8,128)(2,1)S(1)} %copy-done.2), channel_id=1, source_target_pairs={{0,2},{1,7},{2,4},{3,1},{4,6},{5,3},{6,0},{7,5},{8,10},{9,15},{10,... | collective-permute-start | bytes 6291464 | tf_op jit(solution)/shard_map/ppermute | solution.py:38
  113.6 0.7 pad_add_fusion.table
  114.3 2.5 %collective-permute-done.29.far_cross = bf16[4,128,1024]{2,1,0:T(8,128)(2,1)} collective-permute-done((bf16[4,128,1024]{2,1,0:T(8,128)(2,1)}, bf16[4,128,1024]{2,1,0:T(8,128)(2,1)}, u32[]{:S(2)}, u32[]{:S(2)}) %collective-permute-start.29) | collective-permute-done | bytes 1048608 | tf_op jit(solution)/shard_map/ppermute | solution.py:38
  116.9 21.6 %block.3 = (bf16[8,128,1024]{2,1,0:T(8,128)(2,1)}, bf16[8,2,128,128]{3,2,1,0:T(8,128)(2,1)}) custom-call(s32[8]{0:T(128)} %stack.92.order, s32[8,4]{1,0:T(8,128)} %pad_add_fusion.table, bf16[2,4,128,1024]{3,2,1,0:T(8,128)(2,1)} %norm.3.x0.mine, bf16[2,4,128,1024]{3,2,1,0:T(8,128)(2,1)} %collective-permute-done.7.near, ...), custom_call_target="tpu_custom_call" | custom-call | tf_op jit(solution)/shard_map/block/pallas_call | solution.py:303
  138.5 2.3 %slice_bitcast_fusion = bf16[4,128,1024]{2,1,0:T(8,128)(2,1)} fusion(bf16[2,4,128,1024]{3,2,1,0:T(8,128)(2,1)} %collective-permute-done.27.near), kind=kLoop, calls=%fused_computation.4 | loop fusion | bytes 2097152 | tf_op jit(solution)/shard_map/squeeze | solution.py:438
  140.8 1.9 collective-permute-start.31
  142.7 21.7 %block.4 = (bf16[8,128,1024]{2,1,0:T(8,128)(2,1)}, bf16[8,2,128,128]{3,2,1,0:T(8,128)(2,1)}) custom-call(s32[8]{0:T(128)} %stack.92.order, s32[8,4]{1,0:T(8,128)} %pad_add_fusion.table, bf16[2,4,128,1024]{3,2,1,0:T(8,128)(2,1)} %norm.3.x0.mine, ...), custom_call_target="tpu_custom_call", output_to_operand_aliasing={{0}: (18, {}), {1}: (19, {})} | custom-call | tf_op jit(solution)/shard_map/block/pallas_call | solution.py:303
  164.4 0.8 collective-permute-start.32
  165.2 2.3 %collective-permute-done.32.far_cross = bf16[4,128,1024]{2,1,0:T(8,128)(2,1)S(1)} collective-permute-done((bf16[4,128,1024]{2,1,0:T(8,128)(2,1)S(1)}, bf16[4,128,1024]{2,1,0:T(8,128)(2,1)S(1)}, u32[]{:S(2)}, u32[]{:S(2)}) %collective-permute-start.32) | collective-permute-done | bytes 1048608 | tf_op jit(solution)/shard_map/ppermute | solution.py:38
  167.5 1.0 copy-done.13
  168.5 1.3 copy-done.10
  169.8 32.7 %block.5 = (bf16[8,128,1024]{2,1,0:T(8,128)(2,1)}, bf16[8,2,128,128]{3,2,1,0:T(8,128)(2,1)}) custom-call(s32[8]{0:T(128)} %stack.92.order, s32[8,4]{1,0:T(8,128)} %pad_add_fusion.table, bf16[2,4,128,1024]{3,2,1,0:T(8,128)(2,1)} %norm.2.x1.mine, ...), custom_call_target="tpu_custom_call", output_to_operand_aliasing={{0}: (18, {}), {1}: (19, {})} | custom-call | tf_op jit(solution)/shard_map/block/pallas_call | solution.py:303
  (99 shorter events, 6.2 us)
Async XLA Ops:
  0.6 10.3 %copy-start = (bf16[8,128,1024]{2,1,0:T(8,128)(2,1)S(1)}, bf16[8,128,1024]{2,1,0:T(8,128)(2,1)}, u32[]{:S(2)}) copy-start(bf16[8,128,1024]{2,1,0:T(8,128)(2,1)} %own.3) | copy-start | bytes 6291460
  0.6 10.8 %collective-permute-start = (bf16[8,128,1024]{2,1,0:T(8,128)(2,1)}, bf16[8,128,1024]{2,1,0:T(8,128)(2,1)S(1)}, u32[]{:S(2)}, u32[]{:S(2)}) collective-permute-start(bf16[8,128,1024]{2,1,0:T(8,128)(2,1)} %own.3), channel_id=1, source_target_pairs={{0,1},{1,0},{2,3},{3,2},{4,5},{5,4},{6,7},{7,6},{8,9},{9,8},{10,11... | collective-permute-start | bytes 6291464 | tf_op jit(solution)/shard_map/ppermute | solution.py:38
  2.1 4.7 %collective-permute-start.4 = (bf16[256,1024]{1,0:T(8,128)(2,1)}, bf16[256,1024]{1,0:T(8,128)(2,1)S(1)}, u32[]{:S(2)}, u32[]{:S(2)}) collective-permute-start(bf16[256,1024]{1,0:T(8,128)(2,1)} %bitcast.40), channel_id=1, source_target_pairs={{0,1},{1,0},{2,3},{3,2},{4,5},{5,4},{6,7},{7,6},{8,9},{9,8},{10,11... | collective-permute-start | bytes 1572872 | tf_op jit(solution)/shard_map/ppermute | solution.py:38
  8.0 5.2 %copy-start.7 = (bf16[2,256,1024]{2,1,0:T(8,128)(2,1)}, bf16[2,256,1024]{2,1,0:T(8,128)(2,1)S(1)}, u32[]{:S(2)}) copy-start(bf16[2,256,1024]{2,1,0:T(8,128)(2,1)S(1)} %pad_maximum_fusion.mine) | copy-start | bytes 3145732
  8.0 14.7 %collective-permute-start.5 = (bf16[2,256,1024]{2,1,0:T(8,128)(2,1)S(1)}, bf16[2,256,1024]{2,1,0:T(8,128)(2,1)S(1)}, u32[]{:S(2)}, u32[]{:S(2)}) collective-permute-start(bf16[2,256,1024]{2,1,0:T(8,128)(2,1)S(1)} %pad_maximum_fusion.mine), channel_id=1, source_target_pairs={{0,2},{1,7},{2,4},{3,1},{4,6},{5,3},{6,0},{7,5},{8,10},{9,15},{10,... | collective-permute-start | bytes 3145736 | tf_op jit(solution)/shard_map/ppermute | solution.py:38
  11.4 14.6 %copy-start.17 = (bf16[8192]{0:T(1024)(128)(2,1)S(1)}, bf16[8192]{0:T(1024)(128)(2,1)}, u32[]{:S(2)}) copy-start(bf16[8192]{0:T(1024)(128)(2,1)} %param.19) | copy-start | bytes 49156
  13.3 4.1 %collective-permute-start.1 = (f32[8,128]{1,0:T(8,128)S(1)}, f32[8,128]{1,0:T(8,128)S(1)}, u32[]{:S(2)}, u32[]{:S(2)}) collective-permute-start(f32[8,128]{1,0:T(8,128)S(1)} %add.195), channel_id=1, source_target_pairs={{0,6},{1,3},{2,0},{3,5},{4,2},{5,7},{6,4},{7,1},{8,14},{9,11},{10,... | collective-permute-start | bytes 12296 | tf_op jit(solution)/shard_map/ppermute | solution.py:38
  17.4 1.2 collective-permute-start.3
  17.4 4.1 %collective-permute-start.2 = (f32[8,128]{1,0:T(8,128)S(1)}, f32[8,128]{1,0:T(8,128)S(1)}, u32[]{:S(2)}, u32[]{:S(2)}) collective-permute-start(f32[8,128]{1,0:T(8,128)S(1)} %collective-permute-done.1), channel_id=1, source_target_pairs={{0,6},{1,3},{2,0},{3,5},{4,2},{5,7},{6,4},{7,1},{8,14},{9,11},{10,... | collective-permute-start | bytes 12296 | tf_op jit(solution)/shard_map/ppermute | solution.py:38
  22.8 29.7 %copy-start.9 = (bf16[2,256,1024]{2,1,0:T(8,128)(2,1)}, bf16[2,256,1024]{2,1,0:T(8,128)(2,1)S(1)}, u32[]{:S(2)}) copy-start(bf16[2,256,1024]{2,1,0:T(8,128)(2,1)S(1)} %collective-permute-done.5.near) | copy-start | bytes 3145732
  22.8 9.3 %collective-permute-start.6 = (bf16[256,1024]{1,0:T(8,128)(2,1)S(1)}, bf16[256,1024]{1,0:T(8,128)(2,1)}, u32[]{:S(2)}, u32[]{:S(2)}) collective-permute-start(bf16[256,1024]{1,0:T(8,128)(2,1)S(1)} %slice_bitcast_fusion.2), channel_id=1, source_target_pairs={{0,2},{1,7},{2,4},{3,1},{4,6},{5,3},{6,0},{7,5},{8,10},{9,15},{10,... | collective-permute-start | bytes 1572872 | tf_op jit(solution)/shard_map/ppermute | solution.py:38
  27.2 23.5 %collective-permute-start.14 = (bf16[2,256,1024]{2,1,0:T(8,128)(2,1)S(1)}, bf16[2,256,1024]{2,1,0:T(8,128)(2,1)S(1)}, u32[]{:S(2)}, u32[]{:S(2)}) collective-permute-start(bf16[2,256,1024]{2,1,0:T(8,128)(2,1)S(1)} %collective-permute-done.5.near), channel_id=1, source_target_pairs={{0,1},{1,0},{2,3},{3,2},{4,5},{5,4},{6,7},{7,6},{8,9},{9,8},{10,11... | collective-permute-start | bytes 3145736 | tf_op jit(solution)/shard_map/ppermute | solution.py:38
  27.2 8.1 %copy-start.15 = (bf16[4,16,1024]{2,1,0:T(8,128)(2,1)S(1)}, bf16[4,16,1024]{2,1,0:T(8,128)(2,1)}, u32[]{:S(2)}) copy-start(bf16[4,16,1024]{2,1,0:T(8,128)(2,1)} %param.24) | copy-start | bytes 393220
  27.2 8.1 %copy-start.16 = (bf16[4,1024,16]{1,2,0:T(8,128)(2,1)S(1)}, bf16[4,1024,16]{1,2,0:T(8,128)(2,1)}, u32[]{:S(2)}) copy-start(bf16[4,1024,16]{1,2,0:T(8,128)(2,1)} %param.23) | copy-start | bytes 393220
  32.1 60.2 %collective-permute-start.7 = (bf16[2,4,128,1024]{3,2,1,0:T(8,128)(2,1)}, bf16[2,4,128,1024]{3,2,1,0:T(8,128)(2,1)}, u32[]{:S(2)}, u32[]{:S(2)}) collective-permute-start(bf16[2,4,128,1024]{3,2,1,0:T(8,128)(2,1)} %norm.3.x0.mine), channel_id=1, source_target_pairs={{0,2},{1,7},{2,4},{3,1},{4,6},{5,3},{6,0},{7,5},{8,10},{9,15},{10,... | collective-permute-start | bytes 6291464 | tf_op jit(solution)/shard_map/ppermute | solution.py:38
  35.4 7.4 %collective-permute-start.9 = (bf16[4,32,1024]{2,1,0:T(8,128)(2,1)S(1)}, bf16[4,32,1024]{2,1,0:T(8,128)(2,1)S(1)}, u32[]{:S(2)}, u32[]{:S(2)}) collective-permute-start(bf16[4,32,1024]{2,1,0:T(8,128)(2,1)S(1)} %get-tuple-element.44), channel_id=1, source_target_pairs={{0,16},{1,65},{2,18},{3,67},{4,20},{5,69},{6,22},{7,71},{8,24},{9,... | collective-permute-start | bytes 786440 | tf_op jit(solution)/shard_map/ppermute | solution.py:42
  39.1 7.7 %collective-permute-start.8 = (bf16[4,32,1024]{2,1,0:T(8,128)(2,1)S(1)}, bf16[4,32,1024]{2,1,0:T(8,128)(2,1)S(1)}, u32[]{:S(2)}, u32[]{:S(2)}) collective-permute-start(bf16[4,32,1024]{2,1,0:T(8,128)(2,1)S(1)} %get-tuple-element.44), channel_id=1, source_target_pairs={{0,24},{1,97},{2,26},{3,99},{4,28},{5,101},{6,30},{7,103},{8,0},{9... | collective-permute-start | bytes 786440 | tf_op jit(solution)/shard_map/ppermute | solution.py:42
  39.5 7.3 %collective-permute-start.10 = (bf16[4,32,1024]{2,1,0:T(8,128)(2,1)S(1)}, bf16[4,32,1024]{2,1,0:T(8,128)(2,1)S(1)}, u32[]{:S(2)}, u32[]{:S(2)}) collective-permute-start(bf16[4,32,1024]{2,1,0:T(8,128)(2,1)S(1)} %get-tuple-element.44), channel_id=1, source_target_pairs={{0,8},{1,33},{2,10},{3,35},{4,12},{5,37},{6,14},{7,39},{8,16},{9,4... | collective-permute-start | bytes 786440 | tf_op jit(solution)/shard_map/ppermute | solution.py:42
  42.8 9.6 %collective-permute-start.15 = (bf16[256,1024]{1,0:T(8,128)(2,1)}, bf16[256,1024]{1,0:T(8,128)(2,1)}, u32[]{:S(2)}, u32[]{:S(2)}) collective-permute-start(bf16[256,1024]{1,0:T(8,128)(2,1)} %collective-permute-done.6.far), channel_id=1, source_target_pairs={{0,1},{1,0},{2,3},{3,2},{4,5},{5,4},{6,7},{7,6},{8,9},{9,8},{10,11... | collective-permute-start | bytes 1572872 | tf_op jit(solution)/shard_map/ppermute | solution.py:38
  46.9 11.9 %copy-start.8 = (bf16[4,4,32,1024]{3,2,1,0:T(8,128)(2,1)}, bf16[4,4,32,1024]{3,2,1,0:T(8,128)(2,1)S(1)}, u32[]{:S(2)}) copy-start(bf16[4,4,32,1024]{3,2,1,0:T(8,128)(2,1)S(1)} %pad_maximum_fusion.1.a0) | copy-start | bytes 3145732
  47.0 39.4 %collective-permute-start.13 = (bf16[4,4,32,1024]{3,2,1,0:T(8,128)(2,1)S(1)}, bf16[4,4,32,1024]{3,2,1,0:T(8,128)(2,1)}, u32[]{:S(2)}, u32[]{:S(2)}) collective-permute-start(bf16[4,4,32,1024]{3,2,1,0:T(8,128)(2,1)S(1)} %pad_maximum_fusion.1.a0), channel_id=1, source_target_pairs={{0,32},{1,9},{2,34},{3,11},{4,36},{5,13},{6,38},{7,15},{8,40},{9,1... | collective-permute-start | bytes 3145736 | tf_op jit(solution)/shard_map/ppermute | solution.py:42
  48.2 38.2 %collective-permute-start.12 = (bf16[4,4,32,1024]{3,2,1,0:T(8,128)(2,1)S(1)}, bf16[4,4,32,1024]{3,2,1,0:T(8,128)(2,1)}, u32[]{:S(2)}, u32[]{:S(2)}) collective-permute-start(bf16[4,4,32,1024]{3,2,1,0:T(8,128)(2,1)S(1)} %pad_maximum_fusion.1.a0), channel_id=1, source_target_pairs={{0,64},{1,17},{2,66},{3,19},{4,68},{5,21},{6,70},{7,23},{8,72},{9,... | collective-permute-start | bytes 3145736 | tf_op jit(solution)/shard_map/ppermute | solution.py:42
  50.7 35.7 %collective-permute-start.11 = (bf16[4,4,32,1024]{3,2,1,0:T(8,128)(2,1)S(1)}, bf16[4,4,32,1024]{3,2,1,0:T(8,128)(2,1)}, u32[]{:S(2)}, u32[]{:S(2)}) collective-permute-start(bf16[4,4,32,1024]{3,2,1,0:T(8,128)(2,1)S(1)} %pad_maximum_fusion.1.a0), channel_id=1, source_target_pairs={{0,96},{1,25},{2,98},{3,27},{4,100},{5,29},{6,102},{7,31},{8,104},... | collective-permute-start | bytes 3145736 | tf_op jit(solution)/shard_map/ppermute | solution.py:42
  52.4 25.7 %copy-start.20 = (s32[64]{0:T(128)S(1)}, s32[64]{0:T(128)}, u32[]{:S(2)}) copy-start(s32[64]{0:T(128)} %param.25) | copy-start | bytes 772
  52.4 25.7 %copy-start.21 = (s32[8]{0:T(128)S(1)}, s32[8]{0:T(128)}, u32[]{:S(2)}) copy-start(s32[8]{0:T(128)} %param.26) | copy-start | bytes 100
  58.8 6.1 %collective-permute-start.18 = (bf16[2,256,128]{2,1,0:T(8,128)(2,1)}, bf16[2,256,128]{2,1,0:T(8,128)(2,1)S(1)}, u32[]{:S(2)}, u32[]{:S(2)}) collective-permute-start(bf16[2,256,128]{2,1,0:T(8,128)(2,1)} %prefix.1), channel_id=1, source_target_pairs={{0,8},{1,33},{2,10},{3,35},{4,12},{5,37},{6,14},{7,39},{8,16},{9,4... | collective-permute-start | bytes 393224 | tf_op jit(solution)/shard_map/ppermute | solution.py:42
  64.9 15.8 %collective-permute-start.17 = (bf16[2,256,128]{2,1,0:T(8,128)(2,1)}, bf16[2,256,128]{2,1,0:T(8,128)(2,1)S(1)}, u32[]{:S(2)}, u32[]{:S(2)}) collective-permute-start(bf16[2,256,128]{2,1,0:T(8,128)(2,1)} %prefix.1), channel_id=1, source_target_pairs={{0,16},{1,65},{2,18},{3,67},{4,20},{5,69},{6,22},{7,71},{8,24},{9,... | collective-permute-start | bytes 393224 | tf_op jit(solution)/shard_map/ppermute | solution.py:42
  80.7 5.6 %collective-permute-start.16 = (bf16[2,256,128]{2,1,0:T(8,128)(2,1)}, bf16[2,256,128]{2,1,0:T(8,128)(2,1)S(1)}, u32[]{:S(2)}, u32[]{:S(2)}) collective-permute-start(bf16[2,256,128]{2,1,0:T(8,128)(2,1)} %prefix.1), channel_id=1, source_target_pairs={{0,24},{1,97},{2,26},{3,99},{4,28},{5,101},{6,30},{7,103},{8,0},{9... | collective-permute-start | bytes 393224 | tf_op jit(solution)/shard_map/ppermute | solution.py:42
  86.4 7.9 %copy-start.3 = (bf16[4,2,256,128]{3,2,1,0:T(8,128)(2,1)}, bf16[4,2,256,128]{3,2,1,0:T(8,128)(2,1)S(1)}, u32[]{:S(2)}) copy-start(bf16[4,2,256,128]{3,2,1,0:T(8,128)(2,1)S(1)} %pad_maximum_fusion.2.p0) | copy-start | bytes 1572868
  92.2 18.7 %copy-start.2 = (bf16[2,4,128,1024]{3,2,1,0:T(8,128)(2,1)S(1)}, bf16[2,4,128,1024]{3,2,1,0:T(8,128)(2,1)}, u32[]{:S(2)}) copy-start(bf16[2,4,128,1024]{3,2,1,0:T(8,128)(2,1)} %norm.2.x1.mine) | copy-start | bytes 6291460
  92.3 21.0 %copy-start.18 = (s32[8]{0:T(128)S(1)}, s32[8]{0:T(128)}, u32[]{:S(2)}) copy-start(s32[8]{0:T(128)} %param.27) | copy-start | bytes 100
  92.3 21.2 %copy-start.22 = (s32[8,1]{0,1:T(1,128)S(1)}, s32[8,1]{0,1:T(1,128)}, u32[]{:S(2)}) copy-start(s32[8,1]{0,1:T(1,128)} %param.29) | copy-start | bytes 100
  92.3 21.3 %copy-start.19 = (s32[8]{0:T(128)S(1)}, s32[8]{0:T(128)}, u32[]{:S(2)}) copy-start(s32[8]{0:T(128)} %param.28) | copy-start | bytes 100
  93.7 17.2 %collective-permute-start.19 = (bf16[4,128,1024]{2,1,0:T(8,128)(2,1)S(1)}, bf16[4,128,1024]{2,1,0:T(8,128)(2,1)}, u32[]{:S(2)}, u32[]{:S(2)}) collective-permute-start(bf16[4,128,1024]{2,1,0:T(8,128)(2,1)S(1)} %slice_bitcast_fusion.1), channel_id=1, source_target_pairs={{0,2},{1,7},{2,4},{3,1},{4,6},{5,3},{6,0},{7,5},{8,10},{9,15},{10,... | collective-permute-start | bytes 3145736 | tf_op jit(solution)/shard_map/ppermute | solution.py:38
  93.8 17.1 %collective-permute-start.26 = (bf16[4,2,256,128]{3,2,1,0:T(8,128)(2,1)S(1)}, bf16[4,2,256,128]{3,2,1,0:T(8,128)(2,1)S(1)}, u32[]{:S(2)}, u32[]{:S(2)}) collective-permute-start(bf16[4,2,256,128]{3,2,1,0:T(8,128)(2,1)S(1)} %pad_maximum_fusion.2.p0), channel_id=1, source_target_pairs={{0,32},{1,9},{2,34},{3,11},{4,36},{5,13},{6,38},{7,15},{8,40},{9,1... | collective-permute-start | bytes 1572872 | tf_op jit(solution)/shard_map/ppermute | solution.py:42
  94.3 16.7 %collective-permute-start.25 = (bf16[4,2,256,128]{3,2,1,0:T(8,128)(2,1)S(1)}, bf16[4,2,256,128]{3,2,1,0:T(8,128)(2,1)S(1)}, u32[]{:S(2)}, u32[]{:S(2)}) collective-permute-start(bf16[4,2,256,128]{3,2,1,0:T(8,128)(2,1)S(1)} %pad_maximum_fusion.2.p0), channel_id=1, source_target_pairs={{0,64},{1,17},{2,66},{3,19},{4,68},{5,21},{6,70},{7,23},{8,72},{9,... | collective-permute-start | bytes 1572872 | tf_op jit(solution)/shard_map/ppermute | solution.py:42
  94.3 16.7 %collective-permute-start.24 = (bf16[4,2,256,128]{3,2,1,0:T(8,128)(2,1)S(1)}, bf16[4,2,256,128]{3,2,1,0:T(8,128)(2,1)S(1)}, u32[]{:S(2)}, u32[]{:S(2)}) collective-permute-start(bf16[4,2,256,128]{3,2,1,0:T(8,128)(2,1)S(1)} %pad_maximum_fusion.2.p0), channel_id=1, source_target_pairs={{0,96},{1,25},{2,98},{3,27},{4,100},{5,29},{6,102},{7,31},{8,104},... | collective-permute-start | bytes 1572872 | tf_op jit(solution)/shard_map/ppermute | solution.py:42
  96.8 1.5 collective-permute-start.20
  99.1 5.6 %collective-permute-start.21 = (f32[8,16,128]{2,1,0:T(8,128)S(1)}, f32[8,16,128]{2,1,0:T(8,128)S(1)}, u32[]{:S(2)}, u32[]{:S(2)}) collective-permute-start(f32[8,16,128]{2,1,0:T(8,128)S(1)} %add.205), channel_id=1, source_target_pairs={{0,6},{1,3},{2,0},{3,5},{4,2},{5,7},{6,4},{7,1},{8,14},{9,11},{10,... | collective-permute-start | bytes 196616 | tf_op jit(solution)/shard_map/ppermute | solution.py:38
  104.6 1.3 collective-permute-start.23
  105.9 4.3 %collective-permute-start.22 = (f32[8,16,128]{2,1,0:T(8,128)S(1)}, f32[8,16,128]{2,1,0:T(8,128)S(1)}, u32[]{:S(2)}, u32[]{:S(2)}) collective-permute-start(f32[8,16,128]{2,1,0:T(8,128)S(1)} %collective-permute-done.21), channel_id=1, source_target_pairs={{0,6},{1,3},{2,0},{3,5},{4,2},{5,7},{6,4},{7,1},{8,14},{9,11},{10,... | collective-permute-start | bytes 196616 | tf_op jit(solution)/shard_map/ppermute | solution.py:38
  110.8 6.0 %collective-permute-start.28 = (bf16[2,4,128,1024]{3,2,1,0:T(8,128)(2,1)}, bf16[2,4,128,1024]{3,2,1,0:T(8,128)(2,1)}, u32[]{:S(2)}, u32[]{:S(2)}) collective-permute-start(bf16[2,4,128,1024]{3,2,1,0:T(8,128)(2,1)} %collective-permute-done.7.near), channel_id=1, source_target_pairs={{0,1},{1,0},{2,3},{3,2},{4,5},{5,4},{6,7},{7,6},{8,9},{9,8},{10,11... | collective-permute-start | bytes 6291464 | tf_op jit(solution)/shard_map/ppermute | solution.py:38
  110.9 5.9 %copy-start.4 = (bf16[4,2,256,128]{3,2,1,0:T(8,128)(2,1)}, bf16[4,2,256,128]{3,2,1,0:T(8,128)(2,1)S(1)}, u32[]{:S(2)}) copy-start(bf16[4,2,256,128]{3,2,1,0:T(8,128)(2,1)S(1)} %collective-permute-done.26.p3) | copy-start | bytes 1572868
  111.0 27.5 %collective-permute-start.27 = (bf16[2,4,128,1024]{3,2,1,0:T(8,128)(2,1)S(1)}, bf16[2,4,128,1024]{3,2,1,0:T(8,128)(2,1)}, u32[]{:S(2)}, u32[]{:S(2)}) collective-permute-start(bf16[2,4,128,1024]{3,2,1,0:T(8,128)(2,1)S(1)} %copy-done.2), channel_id=1, source_target_pairs={{0,2},{1,7},{2,4},{3,1},{4,6},{5,3},{6,0},{7,5},{8,10},{9,15},{10,... | collective-permute-start | bytes 6291464 | tf_op jit(solution)/shard_map/ppermute | solution.py:38
  113.3 3.6 %collective-permute-start.29 = (bf16[4,128,1024]{2,1,0:T(8,128)(2,1)}, bf16[4,128,1024]{2,1,0:T(8,128)(2,1)}, u32[]{:S(2)}, u32[]{:S(2)}) collective-permute-start(bf16[4,128,1024]{2,1,0:T(8,128)(2,1)} %collective-permute-done.19.far), channel_id=1, source_target_pairs={{0,1},{1,0},{2,3},{3,2},{4,5},{5,4},{6,7},{7,6},{8,9},{9,8},{10,11... | collective-permute-start | bytes 3145736 | tf_op jit(solution)/shard_map/ppermute | solution.py:38
  140.8 23.6 %collective-permute-start.31 = (bf16[4,128,1024]{2,1,0:T(8,128)(2,1)}, bf16[4,128,1024]{2,1,0:T(8,128)(2,1)S(1)}, u32[]{:S(2)}, u32[]{:S(2)}) collective-permute-start(bf16[4,128,1024]{2,1,0:T(8,128)(2,1)} %slice_bitcast_fusion), channel_id=1, source_target_pairs={{0,2},{1,7},{2,4},{3,1},{4,6},{5,3},{6,0},{7,5},{8,10},{9,15},{10,... | collective-permute-start | bytes 3145736 | tf_op jit(solution)/shard_map/ppermute | solution.py:38
  142.7 25.8 %collective-permute-start.30 = (bf16[2,4,128,1024]{3,2,1,0:T(8,128)(2,1)}, bf16[2,4,128,1024]{3,2,1,0:T(8,128)(2,1)S(1)}, u32[]{:S(2)}, u32[]{:S(2)}) collective-permute-start(bf16[2,4,128,1024]{3,2,1,0:T(8,128)(2,1)} %collective-permute-done.27.near), channel_id=1, source_target_pairs={{0,1},{1,0},{2,3},{3,2},{4,5},{5,4},{6,7},{7,6},{8,9},{9,8},{10,11... | collective-permute-start | bytes 6291464 | tf_op jit(solution)/shard_map/ppermute | solution.py:38
  164.4 3.1 %collective-permute-start.32 = (bf16[4,128,1024]{2,1,0:T(8,128)(2,1)S(1)}, bf16[4,128,1024]{2,1,0:T(8,128)(2,1)S(1)}, u32[]{:S(2)}, u32[]{:S(2)}) collective-permute-start(bf16[4,128,1024]{2,1,0:T(8,128)(2,1)S(1)} %collective-permute-done.31.far), channel_id=1, source_target_pairs={{0,1},{1,0},{2,3},{3,2},{4,5},{5,4},{6,7},{7,6},{8,9},{9,8},{10,11... | collective-permute-start | bytes 3145736 | tf_op jit(solution)/shard_map/ppermute | solution.py:38
  (8 other events, 19.0 us)
where the time goes:
time: 204 us; the launch traced here: 203 us
  Pallas kernels  98 us (48%)
  starting transfers between devices  44.8 us (22%)
  waiting for transfers between devices  43.1 us (21%)
  local copies, waits for them, and re-layouts  8.44 us (4%)
  other arithmetic  7.17 us (4%)
    pallas_call x3, Pallas kernels, block_call(): pl.pallas_call(functools.partial(block_kernel, first, start, count), out_...  76 us
    ppermute x21, waiting for transfers between devices, over_tensor(): return lax.ppermute(value, 'tensor', pairs)  29.5 us
    ppermute x12, starting transfers between devices, over_plane(): lax.ppermute(value, ('dp', 'tensor'), plane_shift(k, stage))  26.9 us
    ppermute x21, starting transfers between devices, over_tensor(): return lax.ppermute(value, 'tensor', pairs)  17.9 us
    ppermute x12, waiting for transfers between devices, over_plane(): lax.ppermute(value, ('dp', 'tensor'), plane_shift(k, stage))  13.6 us
    pallas_call x2, Pallas kernels, norm_call(): pl.pallas_call(norm_kernel, out_shape=jax.ShapeDtypeStruct((2, count, seq...  9.81 us
    pallas_call x1, Pallas kernels, prefix_call(): pl.pallas_call(prefix_kernel, out_shape=jax.ShapeDtypeStruct((2, rows, HE...  6.36 us
    pallas_call x1, Pallas kernels, low_call(): pl.pallas_call(low_kernel, out_shape=(jax.ShapeDtypeStruct((requests, RAN...  5.84 us
  transfers between devices with their start and end apart: 33, of which 15 were waited for; matrix products, arithmetic and copies ran while one was open for 4% of the time, Pallas kernels for 32%

commit v1 on v0

--- a/solution.py
+++ b/solution.py
@@ -41,11 +41,6 @@
 def over_plane(value, stage):
     send = lambda k: lax.ppermute(value, ("dp", "tensor"), plane_shift(k, stage))
     return [value, send(-1), send(2), send(1)]
-
-
-def gather_plane(value):
-    first = jnp.stack(over_plane(value, 0))
-    return over_plane(first, 1)
 
 
 def rotate_tables(start, count):
@@ -383,27 +378,29 @@
     prefix = shared_prefix_tokens.reshape(pre, part)
     prefix_other = over_tensor(prefix, SWAP)
     tokens_other = over_tensor(tokens, SWAP)
+    adapter_row = over_plane(
+        jnp.concatenate([adapter_down_weight.transpose(0, 2, 1), adapter_up_weight], axis=1), 0
+    )
     prefix_mine = jnp.stack([prefix, prefix_other])
     prefix_near = over_tensor(prefix_mine, RING)
 
     square = lambda v: jnp.sum(jnp.square(v.astype(F32)), axis=-1)
     chip = square(tokens) + square(tokens_other)
-    one = over_tensor(chip, BACK)
+    adapter_row = jnp.stack(after(adapter_row, chip))
+    adapters = over_plane(adapter_row, 1)
+    one = after((over_tensor(chip, BACK),), adapter_row)[0]
     two = over_tensor(one, BACK)
     mean = (chip + two + one + over_tensor(one, SWAP)) * (1.0 / (8 * part))
     scale = lax.rsqrt(mean + EPS).reshape(requests, 1, seq)
 
     prefix_rest = ring_rest(after((prefix_near,), scale)[0])
-    down, up = after((adapter_down_weight, adapter_up_weight), scale)
-    adapters = gather_plane(jnp.concatenate([down.transpose(0, 2, 1), up], axis=1))
-
     gain = input_norm_gain.astype(F32).reshape(8, 1, part)
     firsts = [sum(CHUNKS[:i]) for i in range(len(CHUNKS))]
     chunks = [
         norm_call(f, n, order[:2], tokens, tokens_other, scale, gain)
         for f, n in zip(firsts, CHUNKS)
     ]
-    near = over_tensor(after(chunks[:1], prefix_rest[2])[0], RING)
+    near = over_tensor(after(chunks[:1], prefix_rest[2], adapters[1], adapters[3])[0], RING)
     pre_cos, pre_sin = rotate_tables(0, pre)
     pair = prefix_call(
         order, prefix_mine, *prefix_rest, gain, key_weight, value_weight, pre_cos, pre_sin

time: 204 us -> 191 us (0.936)
  waiting for transfers between devices: 43.1 us -> 31.7 us
  starting transfers between devices: 44.8 us -> 42.2 us
    ppermute x12, waiting for transfers between devices: 13.6 us -> 4.84 us  [over_plane(): lax.ppermute(value, ('dp', 'tensor'), plane_shift(k, stage))]
    ppermute x12, starting transfers between devices: 26.9 us -> 18.3 us  [over_plane(): lax.ppermute(value, ('dp', 'tensor'), plane_shift(k, stage))]
    ppermute x21, starting transfers between devices: 17.9 us -> 24 us  [over_tensor(): return lax.ppermute(value, 'tensor', pairs)]
    ppermute x21, waiting for transfers between devices: 29.5 us -> 26.8 us  [over_tensor(): return lax.ppermute(value, 'tensor', pairs)]
    unnamed x46 -> x48, local copies, waits for them, and re-layouts: 3.72 us -> 4.18 us
  transfers between devices with their start and end apart: 33 -> 33, of which waited for: 15 -> 13; matrix products, arithmetic and copies ran while one was open for 4% -> 5% of each run, Pallas kernels for 32% -> 34%
where the time goes in v1:
time: 191 us; the launch traced here: 190 us
  Pallas kernels  98.1 us (51%)
  starting transfers between devices  42.2 us (22%)
  waiting for transfers between devices  31.7 us (17%)
  local copies, waits for them, and re-layouts  8.95 us (5%)
  other arithmetic  8.32 us (4%)
    pallas_call x3, Pallas kernels, block_call(): pl.pallas_call(functools.partial(block_kernel, first, start, count), out_...  76.1 us
    ppermute x21, waiting for transfers between devices, over_tensor(): return lax.ppermute(value, 'tensor', pairs)  26.8 us
    ppermute x21, starting transfers between devices, over_tensor(): return lax.ppermute(value, 'tensor', pairs)  24 us
    ppermute x12, starting transfers between devices, over_plane(): lax.ppermute(value, ('dp', 'tensor'), plane_shift(k, stage))  18.3 us
    pallas_call x2, Pallas kernels, norm_call(): pl.pallas_call(norm_kernel, out_shape=jax.ShapeDtypeStruct((2, count, seq...  9.67 us
    pallas_call x1, Pallas kernels, prefix_call(): pl.pallas_call(prefix_kernel, out_shape=jax.ShapeDtypeStruct((2, rows, HE...  6.36 us
    pallas_call x1, Pallas kernels, low_call(): pl.pallas_call(low_kernel, out_shape=(jax.ShapeDtypeStruct((requests, RAN...  5.97 us
    ppermute x12, waiting for transfers between devices, over_plane(): lax.ppermute(value, ('dp', 'tensor'), plane_shift(k, stage))  4.84 us
  transfers between devices with their start and end apart: 33, of which 13 were waited for; matrix products, arithmetic and copies ran while one was open for 5% of the time, Pallas kernels for 34%

profile of v1, /device:TPU:1, one launch (start us, length us, event | category | flops | bytes accessed | tf_op | source)
XLA Modules:
  0.0 190.4 jit_solution(17844151160722323120)
XLA Ops:
  0.6 1.5 collective-permute-start
  2.2 4.7 %collective-permute-done.7 = bf16[256,1024]{1,0:T(8,128)(2,1)S(1)} collective-permute-done((bf16[256,1024]{1,0:T(8,128)(2,1)}, bf16[256,1024]{1,0:T(8,128)(2,1)S(1)}, u32[]{:S(2)}, u32[]{:S(2)}) %collective-permute-start.7) | collective-permute-done | bytes 524320 | tf_op jit(solution)/shard_map/ppermute | solution.py:38
  6.9 1.1 pad_maximum_fusion.1.mine
  8.0 2.9 %collective-permute-start.8 = (bf16[2,256,1024]{2,1,0:T(8,128)(2,1)S(1)}, bf16[2,256,1024]{2,1,0:T(8,128)(2,1)S(1)}, u32[]{:S(2)}, u32[]{:S(2)}) collective-permute-start(bf16[2,256,1024]{2,1,0:T(8,128)(2,1)S(1)} %pad_maximum_fusion.1.mine), channel_id=1, source_target_pairs={{0,2},{1,7},{2,4},{3,1},{4,6},{5,3},{6,0},{7,5},{8,10},{9,15},{10,... | collective-permute-start | bytes 3145736 | tf_op jit(solution)/shard_map/ppermute | solution.py:38
  10.9 1.0 pad_maximum_fusion.3
  11.9 1.7 collective-permute-start.4
  13.6 3.3 %collective-permute-start.3 = (bf16[4,32,1024]{2,1,0:T(8,128)(2,1)S(1)}, bf16[4,32,1024]{2,1,0:T(8,128)(2,1)S(1)}, u32[]{:S(2)}, u32[]{:S(2)}) collective-permute-start(bf16[4,32,1024]{2,1,0:T(8,128)(2,1)S(1)} %pad_maximum_fusion.3), channel_id=1, source_target_pairs={{0,16},{1,65},{2,18},{3,67},{4,20},{5,69},{6,22},{7,71},{8,24},{9,... | collective-permute-start | bytes 786440 | tf_op jit(solution)/shard_map/ppermute | solution.py:42
  18.7 1.1 collective-permute-done.4
  19.8 3.7 %collective-permute-done.3 = bf16[4,32,1024]{2,1,0:T(8,128)(2,1)S(1)} collective-permute-done((bf16[4,32,1024]{2,1,0:T(8,128)(2,1)S(1)}, bf16[4,32,1024]{2,1,0:T(8,128)(2,1)S(1)}, u32[]{:S(2)}, u32[]{:S(2)}) %collective-permute-start.3) | collective-permute-done | bytes 262176 | tf_op jit(solution)/shard_map/ppermute | solution.py:42
  23.7 1.3 collective-permute-start.11
  24.9 1.5 collective-permute-start.10
  26.4 4.1 %collective-permute-done.1 = f32[8,128]{1,0:T(8,128)S(1)} collective-permute-done((f32[8,128]{1,0:T(8,128)S(1)}, f32[8,128]{1,0:T(8,128)S(1)}, u32[]{:S(2)}, u32[]{:S(2)}) %collective-permute-start.1) | collective-permute-done | bytes 4128 | tf_op jit(solution)/shard_map/ppermute | solution.py:38
  30.5 1.3 collective-permute-start.5
  31.8 2.8 %collective-permute-done.5 = f32[8,128]{1,0:T(8,128)S(1)} collective-permute-done((f32[8,128]{1,0:T(8,128)S(1)}, f32[8,128]{1,0:T(8,128)S(1)}, u32[]{:S(2)}, u32[]{:S(2)}) %collective-permute-start.5) | collective-permute-done | bytes 4128 | tf_op jit(solution)/shard_map/ppermute | solution.py:38
  35.2 1.0 copy-done.9
  36.2 1.5 collective-permute-start.9
  39.0 4.9 %norm.3.x0.mine = bf16[2,4,128,1024]{3,2,1,0:T(8,128)(2,1)} custom-call(s32[2]{0:T(128)} %pad_add_fusion.2.place, bf16[8,128,1024]{2,1,0:T(8,128)(2,1)} %own.3, bf16[8,128,1024]{2,1,0:T(8,128)(2,1)} %copy-done.1, f32[8,1,128]{2,1,0:T(1,128)} %bitcast.48, f32[8,1,1024]{2,1,0:T(1,128)} %bitcast.33, f32[8,1,1024]{2,1,0:T(1,128)} %bitcast.34), custom_call_target="tpu_custom_call" | custom-call | tf_op jit(solution)/shard_map/norm/pallas_call | solution.py:79
  44.6 0.8 copy-done.16
  45.4 2.4 %collective-permute-start.12 = (bf16[2,4,128,1024]{3,2,1,0:T(8,128)(2,1)}, bf16[2,4,128,1024]{3,2,1,0:T(8,128)(2,1)}, u32[]{:S(2)}, u32[]{:S(2)}) collective-permute-start(bf16[2,4,128,1024]{3,2,1,0:T(8,128)(2,1)} %norm.3.x0.mine), channel_id=1, source_target_pairs={{0,2},{1,7},{2,4},{3,1},{4,6},{5,3},{6,0},{7,5},{8,10},{9,15},{10,... | collective-permute-start | bytes 6291464 | tf_op jit(solution)/shard_map/ppermute | solution.py:38
  47.9 2.7 %collective-permute-start.13 = (bf16[4,4,32,1024]{3,2,1,0:T(8,128)(2,1)S(1)}, bf16[4,4,32,1024]{3,2,1,0:T(8,128)(2,1)}, u32[]{:S(2)}, u32[]{:S(2)}) collective-permute-start(bf16[4,4,32,1024]{3,2,1,0:T(8,128)(2,1)S(1)} %pad_maximum_fusion.a0), channel_id=1, source_target_pairs={{0,64},{1,17},{2,66},{3,19},{4,68},{5,21},{6,70},{7,23},{8,72},{9,... | collective-permute-start | bytes 3145736 | tf_op jit(solution)/shard_map/ppermute | solution.py:42
  51.5 1.4 collective-permute-done.15.far_cross
  52.9 6.4 %prefix.1 = bf16[2,256,128]{2,1,0:T(8,128)(2,1)} custom-call(s32[8]{0:T(128)} %stack.92.order, bf16[2,256,1024]{2,1,0:T(8,128)(2,1)} %copy-done.7, bf16[2,256,1024]{2,1,0:T(8,128)(2,1)} %copy-done.9, bf16[2,256,1024]{2,1,0:T(8,128)(2,1)} %copy-done.12, bf16[256,1024]{1,0:T(8,128)(2,1)} %copy-done.16, bf16[256,1024]{1,0:T(8,128)(2,1)} %collective-permute-done.15.far_cross, ...), custom_call_target="tpu_custom_call" | custom-call | tf_op jit(solution)/shard_map/prefix/pallas_call | solution.py:120
  59.2 2.8 %collective-permute-start.17 = (bf16[2,256,128]{2,1,0:T(8,128)(2,1)}, bf16[2,256,128]{2,1,0:T(8,128)(2,1)S(1)}, u32[]{:S(2)}, u32[]{:S(2)}) collective-permute-start(bf16[2,256,128]{2,1,0:T(8,128)(2,1)} %prefix.1), channel_id=1, source_target_pairs={{0,16},{1,65},{2,18},{3,67},{4,20},{5,69},{6,22},{7,71},{8,24},{9,... | collective-permute-start | bytes 393224 | tf_op jit(solution)/shard_map/ppermute | solution.py:42
  63.5 4.8 %norm.2.x1.mine = bf16[2,4,128,1024]{3,2,1,0:T(8,128)(2,1)} custom-call(s32[2]{0:T(128)} %pad_add_fusion.2.place, bf16[8,128,1024]{2,1,0:T(8,128)(2,1)} %own.3, bf16[8,128,1024]{2,1,0:T(8,128)(2,1)} %copy-done.1, f32[8,1,128]{2,1,0:T(1,128)} %bitcast.49, f32[8,1,1024]{2,1,0:T(1,128)} %bitcast.36, f32[8,1,1024]{2,1,0:T(1,128)} %bitcast.37), custom_call_target="tpu_custom_call" | custom-call | tf_op jit(solution)/shard_map/norm/pallas_call | solution.py:79
  68.3 6.0 %low.1 = (f32[8,16,128]{2,1,0:T(8,128)}, bf16[8,16,1024]{2,1,0:T(8,128)(2,1)}) custom-call(s32[8,3]{1,0:T(8,128)} %pad_add_fusion.1.pick, bf16[2,4,128,1024]{3,2,1,0:T(8,128)(2,1)} %norm.3.x0.mine, bf16[2,4,128,1024]{3,2,1,0:T(8,128)(2,1)} %norm.2.x1.mine, bf16[4,4,32,1024]{3,2,1,0:T(8,128)(2,1)} %copy-done.8, ...), custom_call_target="tpu_custom_call" | custom-call | tf_op jit(solution)/shard_map/low/pallas_call | solution.py:156
  74.4 1.1 pad_maximum_fusion.2.p0
  75.5 1.5 slice_bitcast_fusion.1
  77.0 3.0 %collective-permute-start.19 = (bf16[4,128,1024]{2,1,0:T(8,128)(2,1)S(1)}, bf16[4,128,1024]{2,1,0:T(8,128)(2,1)}, u32[]{:S(2)}, u32[]{:S(2)}) collective-permute-start(bf16[4,128,1024]{2,1,0:T(8,128)(2,1)S(1)} %slice_bitcast_fusion.1), channel_id=1, source_target_pairs={{0,2},{1,7},{2,4},{3,1},{4,6},{5,3},{6,0},{7,5},{8,10},{9,15},{10,... | collective-permute-start | bytes 3145736 | tf_op jit(solution)/shard_map/ppermute | solution.py:38
  80.4 2.1 %collective-permute-start.25 = (bf16[4,2,256,128]{3,2,1,0:T(8,128)(2,1)S(1)}, bf16[4,2,256,128]{3,2,1,0:T(8,128)(2,1)S(1)}, u32[]{:S(2)}, u32[]{:S(2)}) collective-permute-start(bf16[4,2,256,128]{3,2,1,0:T(8,128)(2,1)S(1)} %pad_maximum_fusion.2.p0), channel_id=1, source_target_pairs={{0,64},{1,17},{2,66},{3,19},{4,68},{5,21},{6,70},{7,23},{8,72},{9,... | collective-permute-start | bytes 1572872 | tf_op jit(solution)/shard_map/ppermute | solution.py:42
  82.5 1.0 collective-permute-start.24
  83.6 1.2 collective-permute-done.20
  84.8 2.0 %collective-permute-start.21 = (f32[8,16,128]{2,1,0:T(8,128)S(1)}, f32[8,16,128]{2,1,0:T(8,128)S(1)}, u32[]{:S(2)}, u32[]{:S(2)}) collective-permute-start(f32[8,16,128]{2,1,0:T(8,128)S(1)} %add.205), channel_id=1, source_target_pairs={{0,6},{1,3},{2,0},{3,5},{4,2},{5,7},{6,4},{7,1},{8,14},{9,11},{10,... | collective-permute-start | bytes 196616 | tf_op jit(solution)/shard_map/ppermute | solution.py:38
  86.8 3.6 %collective-permute-done.21 = f32[8,16,128]{2,1,0:T(8,128)S(1)} collective-permute-done((f32[8,16,128]{2,1,0:T(8,128)S(1)}, f32[8,16,128]{2,1,0:T(8,128)S(1)}, u32[]{:S(2)}, u32[]{:S(2)}) %collective-permute-start.21) | collective-permute-done | bytes 65568 | tf_op jit(solution)/shard_map/ppermute | solution.py:38
  90.4 1.2 collective-permute-done.23
  91.6 1.4 collective-permute-start.22
  93.1 2.9 %collective-permute-done.22 = f32[8,16,128]{2,1,0:T(8,128)S(1)} collective-permute-done((f32[8,16,128]{2,1,0:T(8,128)S(1)}, f32[8,16,128]{2,1,0:T(8,128)S(1)}, u32[]{:S(2)}, u32[]{:S(2)}) %collective-permute-start.22) | collective-permute-done | bytes 65568 | tf_op jit(solution)/shard_map/ppermute | solution.py:38
  96.6 0.9 collective-permute-start.28
  97.6 3.4 %collective-permute-start.27 = (bf16[2,4,128,1024]{3,2,1,0:T(8,128)(2,1)S(1)}, bf16[2,4,128,1024]{3,2,1,0:T(8,128)(2,1)}, u32[]{:S(2)}, u32[]{:S(2)}) collective-permute-start(bf16[2,4,128,1024]{3,2,1,0:T(8,128)(2,1)S(1)} %copy-done.2), channel_id=1, source_target_pairs={{0,2},{1,7},{2,4},{3,1},{4,6},{5,3},{6,0},{7,5},{8,10},{9,15},{10,... | collective-permute-start | bytes 6291464 | tf_op jit(solution)/shard_map/ppermute | solution.py:38
  102.0 1.9 %collective-permute-done.29.far_cross = bf16[4,128,1024]{2,1,0:T(8,128)(2,1)} collective-permute-done((bf16[4,128,1024]{2,1,0:T(8,128)(2,1)}, bf16[4,128,1024]{2,1,0:T(8,128)(2,1)}, u32[]{:S(2)}, u32[]{:S(2)}) %collective-permute-start.29) | collective-permute-done | bytes 1048608 | tf_op jit(solution)/shard_map/ppermute | solution.py:38
  103.9 21.7 %block.3 = (bf16[8,128,1024]{2,1,0:T(8,128)(2,1)}, bf16[8,2,128,128]{3,2,1,0:T(8,128)(2,1)}) custom-call(s32[8]{0:T(128)} %stack.92.order, s32[8,4]{1,0:T(8,128)} %pad_add_fusion.table, bf16[2,4,128,1024]{3,2,1,0:T(8,128)(2,1)} %norm.3.x0.mine, bf16[2,4,128,1024]{3,2,1,0:T(8,128)(2,1)} %collective-permute-done.12.near, ...), custom_call_target="tpu_custom_call" | custom-call | tf_op jit(solution)/shard_map/block/pallas_call | solution.py:298
  125.6 2.3 %slice_bitcast_fusion = bf16[4,128,1024]{2,1,0:T(8,128)(2,1)} fusion(bf16[2,4,128,1024]{3,2,1,0:T(8,128)(2,1)} %collective-permute-done.27.near), kind=kLoop, calls=%fused_computation.4 | loop fusion | bytes 2097152 | tf_op jit(solution)/shard_map/squeeze | solution.py:435
  127.9 2.5 %collective-permute-start.31 = (bf16[4,128,1024]{2,1,0:T(8,128)(2,1)}, bf16[4,128,1024]{2,1,0:T(8,128)(2,1)S(1)}, u32[]{:S(2)}, u32[]{:S(2)}) collective-permute-start(bf16[4,128,1024]{2,1,0:T(8,128)(2,1)} %slice_bitcast_fusion), channel_id=1, source_target_pairs={{0,2},{1,7},{2,4},{3,1},{4,6},{5,3},{6,0},{7,5},{8,10},{9,15},{10,... | collective-permute-start | bytes 3145736 | tf_op jit(solution)/shard_map/ppermute | solution.py:38
  130.4 21.7 %block.4 = (bf16[8,128,1024]{2,1,0:T(8,128)(2,1)}, bf16[8,2,128,128]{3,2,1,0:T(8,128)(2,1)}) custom-call(s32[8]{0:T(128)} %stack.92.order, s32[8,4]{1,0:T(8,128)} %pad_add_fusion.table, bf16[2,4,128,1024]{3,2,1,0:T(8,128)(2,1)} %norm.3.x0.mine, ...), custom_call_target="tpu_custom_call", output_to_operand_aliasing={{0}: (18, {}), {1}: (19, {})} | custom-call | tf_op jit(solution)/shard_map/block/pallas_call | solution.py:298
  152.1 0.8 collective-permute-start.32
  152.9 2.3 %collective-permute-done.32.far_cross = bf16[4,128,1024]{2,1,0:T(8,128)(2,1)S(1)} collective-permute-done((bf16[4,128,1024]{2,1,0:T(8,128)(2,1)S(1)}, bf16[4,128,1024]{2,1,0:T(8,128)(2,1)S(1)}, u32[]{:S(2)}, u32[]{:S(2)}) %collective-permute-start.32) | collective-permute-done | bytes 1048608 | tf_op jit(solution)/shard_map/ppermute | solution.py:38
  155.2 1.0 copy-done.14
  156.2 1.3 copy-done.11
  157.5 32.7 %block.5 = (bf16[8,128,1024]{2,1,0:T(8,128)(2,1)}, bf16[8,2,128,128]{3,2,1,0:T(8,128)(2,1)}) custom-call(s32[8]{0:T(128)} %stack.92.order, s32[8,4]{1,0:T(8,128)} %pad_add_fusion.table, bf16[2,4,128,1024]{3,2,1,0:T(8,128)(2,1)} %norm.2.x1.mine, ...), custom_call_target="tpu_custom_call", output_to_operand_aliasing={{0}: (18, {}), {1}: (19, {})} | custom-call | tf_op jit(solution)/shard_map/block/pallas_call | solution.py:298
  (101 shorter events, 9.3 us)
Async XLA Ops:
  0.6 17.0 %copy-start = (bf16[8,128,1024]{2,1,0:T(8,128)(2,1)S(1)}, bf16[8,128,1024]{2,1,0:T(8,128)(2,1)}, u32[]{:S(2)}) copy-start(bf16[8,128,1024]{2,1,0:T(8,128)(2,1)} %own.3) | copy-start | bytes 6291460
  0.6 17.5 %collective-permute-start = (bf16[8,128,1024]{2,1,0:T(8,128)(2,1)}, bf16[8,128,1024]{2,1,0:T(8,128)(2,1)S(1)}, u32[]{:S(2)}, u32[]{:S(2)}) collective-permute-start(bf16[8,128,1024]{2,1,0:T(8,128)(2,1)} %own.3), channel_id=1, source_target_pairs={{0,1},{1,0},{2,3},{3,2},{4,5},{5,4},{6,7},{7,6},{8,9},{9,8},{10,11... | collective-permute-start | bytes 6291464 | tf_op jit(solution)/shard_map/ppermute | solution.py:38
  2.1 4.7 %collective-permute-start.7 = (bf16[256,1024]{1,0:T(8,128)(2,1)}, bf16[256,1024]{1,0:T(8,128)(2,1)S(1)}, u32[]{:S(2)}, u32[]{:S(2)}) collective-permute-start(bf16[256,1024]{1,0:T(8,128)(2,1)} %bitcast.40), channel_id=1, source_target_pairs={{0,1},{1,0},{2,3},{3,2},{4,5},{5,4},{6,7},{7,6},{8,9},{9,8},{10,11... | collective-permute-start | bytes 1572872 | tf_op jit(solution)/shard_map/ppermute | solution.py:38
  8.0 10.6 %copy-start.7 = (bf16[2,256,1024]{2,1,0:T(8,128)(2,1)}, bf16[2,256,1024]{2,1,0:T(8,128)(2,1)S(1)}, u32[]{:S(2)}) copy-start(bf16[2,256,1024]{2,1,0:T(8,128)(2,1)S(1)} %pad_maximum_fusion.1.mine) | copy-start | bytes 3145732
  8.0 27.2 %collective-permute-start.8 = (bf16[2,256,1024]{2,1,0:T(8,128)(2,1)S(1)}, bf16[2,256,1024]{2,1,0:T(8,128)(2,1)S(1)}, u32[]{:S(2)}, u32[]{:S(2)}) collective-permute-start(bf16[2,256,1024]{2,1,0:T(8,128)(2,1)S(1)} %pad_maximum_fusion.1.mine), channel_id=1, source_target_pairs={{0,2},{1,7},{2,4},{3,1},{4,6},{5,3},{6,0},{7,5},{8,10},{9,15},{10,... | collective-permute-start | bytes 3145736 | tf_op jit(solution)/shard_map/ppermute | solution.py:38
  11.9 7.9 %collective-permute-start.4 = (bf16[4,32,1024]{2,1,0:T(8,128)(2,1)S(1)}, bf16[4,32,1024]{2,1,0:T(8,128)(2,1)S(1)}, u32[]{:S(2)}, u32[]{:S(2)}) collective-permute-start(bf16[4,32,1024]{2,1,0:T(8,128)(2,1)S(1)} %pad_maximum_fusion.3), channel_id=1, source_target_pairs={{0,8},{1,33},{2,10},{3,35},{4,12},{5,37},{6,14},{7,39},{8,16},{9,4... | collective-permute-start | bytes 786440 | tf_op jit(solution)/shard_map/ppermute | solution.py:42
  13.6 9.9 %collective-permute-start.3 = (bf16[4,32,1024]{2,1,0:T(8,128)(2,1)S(1)}, bf16[4,32,1024]{2,1,0:T(8,128)(2,1)S(1)}, u32[]{:S(2)}, u32[]{:S(2)}) collective-permute-start(bf16[4,32,1024]{2,1,0:T(8,128)(2,1)S(1)} %pad_maximum_fusion.3), channel_id=1, source_target_pairs={{0,16},{1,65},{2,18},{3,67},{4,20},{5,69},{6,22},{7,71},{8,24},{9,... | collective-permute-start | bytes 786440 | tf_op jit(solution)/shard_map/ppermute | solution.py:42
  16.9 6.6 %collective-permute-start.2 = (bf16[4,32,1024]{2,1,0:T(8,128)(2,1)S(1)}, bf16[4,32,1024]{2,1,0:T(8,128)(2,1)S(1)}, u32[]{:S(2)}, u32[]{:S(2)}) collective-permute-start(bf16[4,32,1024]{2,1,0:T(8,128)(2,1)S(1)} %pad_maximum_fusion.3), channel_id=1, source_target_pairs={{0,24},{1,97},{2,26},{3,99},{4,28},{5,101},{6,30},{7,103},{8,0},{9... | collective-permute-start | bytes 786440 | tf_op jit(solution)/shard_map/ppermute | solution.py:42
  18.7 19.1 %copy-start.18 = (bf16[8192]{0:T(1024)(128)(2,1)S(1)}, bf16[8192]{0:T(1024)(128)(2,1)}, u32[]{:S(2)}) copy-start(bf16[8192]{0:T(1024)(128)(2,1)} %param.19) | copy-start | bytes 49156
  23.6 24.3 %copy-start.8 = (bf16[4,4,32,1024]{3,2,1,0:T(8,128)(2,1)}, bf16[4,4,32,1024]{3,2,1,0:T(8,128)(2,1)S(1)}, u32[]{:S(2)}) copy-start(bf16[4,4,32,1024]{3,2,1,0:T(8,128)(2,1)S(1)} %pad_maximum_fusion.a0) | copy-start | bytes 3145732
  23.7 21.0 %collective-permute-start.11 = (bf16[4,4,32,1024]{3,2,1,0:T(8,128)(2,1)S(1)}, bf16[4,4,32,1024]{3,2,1,0:T(8,128)(2,1)}, u32[]{:S(2)}, u32[]{:S(2)}) collective-permute-start(bf16[4,4,32,1024]{3,2,1,0:T(8,128)(2,1)S(1)} %pad_maximum_fusion.a0), channel_id=1, source_target_pairs={{0,32},{1,9},{2,34},{3,11},{4,36},{5,13},{6,38},{7,15},{8,40},{9,1... | collective-permute-start | bytes 3145736 | tf_op jit(solution)/shard_map/ppermute | solution.py:42
  24.9 19.7 %collective-permute-start.10 = (bf16[4,4,32,1024]{3,2,1,0:T(8,128)(2,1)S(1)}, bf16[4,4,32,1024]{3,2,1,0:T(8,128)(2,1)}, u32[]{:S(2)}, u32[]{:S(2)}) collective-permute-start(bf16[4,4,32,1024]{3,2,1,0:T(8,128)(2,1)S(1)} %pad_maximum_fusion.a0), channel_id=1, source_target_pairs={{0,96},{1,25},{2,98},{3,27},{4,100},{5,29},{6,102},{7,31},{8,104},... | collective-permute-start | bytes 3145736 | tf_op jit(solution)/shard_map/ppermute | solution.py:42
  26.4 4.1 %collective-permute-start.1 = (f32[8,128]{1,0:T(8,128)S(1)}, f32[8,128]{1,0:T(8,128)S(1)}, u32[]{:S(2)}, u32[]{:S(2)}) collective-permute-start(f32[8,128]{1,0:T(8,128)S(1)} %add.195), channel_id=1, source_target_pairs={{0,6},{1,3},{2,0},{3,5},{4,2},{5,7},{6,4},{7,1},{8,14},{9,11},{10,... | collective-permute-start | bytes 12296 | tf_op jit(solution)/shard_map/ppermute | solution.py:38
  30.5 1.4 collective-permute-start.6
  30.5 4.1 %collective-permute-start.5 = (f32[8,128]{1,0:T(8,128)S(1)}, f32[8,128]{1,0:T(8,128)S(1)}, u32[]{:S(2)}, u32[]{:S(2)}) collective-permute-start(f32[8,128]{1,0:T(8,128)S(1)} %collective-permute-done.1), channel_id=1, source_target_pairs={{0,6},{1,3},{2,0},{3,5},{4,2},{5,7},{6,4},{7,1},{8,14},{9,11},{10,... | collective-permute-start | bytes 12296 | tf_op jit(solution)/shard_map/ppermute | solution.py:38
  36.2 8.4 %collective-permute-start.9 = (bf16[256,1024]{1,0:T(8,128)(2,1)S(1)}, bf16[256,1024]{1,0:T(8,128)(2,1)S(1)}, u32[]{:S(2)}, u32[]{:S(2)}) collective-permute-start(bf16[256,1024]{1,0:T(8,128)(2,1)S(1)} %slice_bitcast_fusion.2), channel_id=1, source_target_pairs={{0,2},{1,7},{2,4},{3,1},{4,6},{5,3},{6,0},{7,5},{8,10},{9,15},{10,... | collective-permute-start | bytes 1572872 | tf_op jit(solution)/shard_map/ppermute | solution.py:38
  38.9 8.8 %copy-start.10 = (bf16[2,256,1024]{2,1,0:T(8,128)(2,1)S(1)}, bf16[2,256,1024]{2,1,0:T(8,128)(2,1)}, u32[]{:S(2)}) copy-start(bf16[2,256,1024]{2,1,0:T(8,128)(2,1)} %copy-done.9) | copy-start | bytes 3145732
  38.9 11.7 %copy-start.21 = (s32[64]{0:T(128)S(1)}, s32[64]{0:T(128)}, u32[]{:S(2)}) copy-start(s32[64]{0:T(128)} %param.25) | copy-start | bytes 772
  38.9 11.7 %copy-start.22 = (s32[8]{0:T(128)S(1)}, s32[8]{0:T(128)}, u32[]{:S(2)}) copy-start(s32[8]{0:T(128)} %param.26) | copy-start | bytes 100
  45.4 30.1 %collective-permute-start.12 = (bf16[2,4,128,1024]{3,2,1,0:T(8,128)(2,1)}, bf16[2,4,128,1024]{3,2,1,0:T(8,128)(2,1)}, u32[]{:S(2)}, u32[]{:S(2)}) collective-permute-start(bf16[2,4,128,1024]{3,2,1,0:T(8,128)(2,1)} %norm.3.x0.mine), channel_id=1, source_target_pairs={{0,2},{1,7},{2,4},{3,1},{4,6},{5,3},{6,0},{7,5},{8,10},{9,15},{10,... | collective-permute-start | bytes 6291464 | tf_op jit(solution)/shard_map/ppermute | solution.py:38
  47.8 3.7 %collective-permute-start.14 = (bf16[2,256,1024]{2,1,0:T(8,128)(2,1)S(1)}, bf16[2,256,1024]{2,1,0:T(8,128)(2,1)S(1)}, u32[]{:S(2)}, u32[]{:S(2)}) collective-permute-start(bf16[2,256,1024]{2,1,0:T(8,128)(2,1)S(1)} %copy-done.10), channel_id=1, source_target_pairs={{0,1},{1,0},{2,3},{3,2},{4,5},{5,4},{6,7},{7,6},{8,9},{9,8},{10,11... | collective-permute-start | bytes 3145736 | tf_op jit(solution)/shard_map/ppermute | solution.py:38
  47.9 20.3 %collective-permute-start.13 = (bf16[4,4,32,1024]{3,2,1,0:T(8,128)(2,1)S(1)}, bf16[4,4,32,1024]{3,2,1,0:T(8,128)(2,1)}, u32[]{:S(2)}, u32[]{:S(2)}) collective-permute-start(bf16[4,4,32,1024]{3,2,1,0:T(8,128)(2,1)S(1)} %pad_maximum_fusion.a0), channel_id=1, source_target_pairs={{0,64},{1,17},{2,66},{3,19},{4,68},{5,21},{6,70},{7,23},{8,72},{9,... | collective-permute-start | bytes 3145736 | tf_op jit(solution)/shard_map/ppermute | solution.py:42
  50.6 2.3 %collective-permute-start.15 = (bf16[256,1024]{1,0:T(8,128)(2,1)}, bf16[256,1024]{1,0:T(8,128)(2,1)}, u32[]{:S(2)}, u32[]{:S(2)}) collective-permute-start(bf16[256,1024]{1,0:T(8,128)(2,1)} %copy-done.16), channel_id=1, source_target_pairs={{0,1},{1,0},{2,3},{3,2},{4,5},{5,4},{6,7},{7,6},{8,9},{9,8},{10,11... | collective-permute-start | bytes 1572872 | tf_op jit(solution)/shard_map/ppermute | solution.py:38
  59.2 15.1 %collective-permute-start.18 = (bf16[2,256,128]{2,1,0:T(8,128)(2,1)}, bf16[2,256,128]{2,1,0:T(8,128)(2,1)S(1)}, u32[]{:S(2)}, u32[]{:S(2)}) collective-permute-start(bf16[2,256,128]{2,1,0:T(8,128)(2,1)} %prefix.1), channel_id=1, source_target_pairs={{0,8},{1,33},{2,10},{3,35},{4,12},{5,37},{6,14},{7,39},{8,16},{9,4... | collective-permute-start | bytes 393224 | tf_op jit(solution)/shard_map/ppermute | solution.py:42
  59.2 15.1 %collective-permute-start.17 = (bf16[2,256,128]{2,1,0:T(8,128)(2,1)}, bf16[2,256,128]{2,1,0:T(8,128)(2,1)S(1)}, u32[]{:S(2)}, u32[]{:S(2)}) collective-permute-start(bf16[2,256,128]{2,1,0:T(8,128)(2,1)} %prefix.1), channel_id=1, source_target_pairs={{0,16},{1,65},{2,18},{3,67},{4,20},{5,69},{6,22},{7,71},{8,24},{9,... | collective-permute-start | bytes 393224 | tf_op jit(solution)/shard_map/ppermute | solution.py:42
  62.1 12.3 %collective-permute-start.16 = (bf16[2,256,128]{2,1,0:T(8,128)(2,1)}, bf16[2,256,128]{2,1,0:T(8,128)(2,1)}, u32[]{:S(2)}, u32[]{:S(2)}) collective-permute-start(bf16[2,256,128]{2,1,0:T(8,128)(2,1)} %prefix.1), channel_id=1, source_target_pairs={{0,24},{1,97},{2,26},{3,99},{4,28},{5,101},{6,30},{7,103},{8,0},{9... | collective-permute-start | bytes 393224 | tf_op jit(solution)/shard_map/ppermute | solution.py:42
  68.3 6.1 %copy-start.15 = (bf16[2,256,128]{2,1,0:T(8,128)(2,1)S(1)}, bf16[2,256,128]{2,1,0:T(8,128)(2,1)}, u32[]{:S(2)}) copy-start(bf16[2,256,128]{2,1,0:T(8,128)(2,1)} %prefix.1) | copy-start | bytes 393220
  74.3 9.3 %copy-start.17 = (f32[8,16,128]{2,1,0:T(8,128)S(1)}, f32[8,16,128]{2,1,0:T(8,128)}, u32[]{:S(2)}) copy-start(f32[8,16,128]{2,1,0:T(8,128)} %get-tuple-element.31) | copy-start | bytes 196612
  74.3 23.3 %copy-start.2 = (bf16[2,4,128,1024]{3,2,1,0:T(8,128)(2,1)S(1)}, bf16[2,4,128,1024]{3,2,1,0:T(8,128)(2,1)}, u32[]{:S(2)}) copy-start(bf16[2,4,128,1024]{3,2,1,0:T(8,128)(2,1)} %norm.2.x1.mine) | copy-start | bytes 6291460
  74.3 26.7 %copy-start.19 = (s32[8]{0:T(128)S(1)}, s32[8]{0:T(128)}, u32[]{:S(2)}) copy-start(s32[8]{0:T(128)} %param.27) | copy-start | bytes 100
  74.3 26.9 %copy-start.23 = (s32[8,1]{0,1:T(1,128)S(1)}, s32[8,1]{0,1:T(1,128)}, u32[]{:S(2)}) copy-start(s32[8,1]{0,1:T(1,128)} %param.29) | copy-start | bytes 100
  74.3 26.9 %copy-start.20 = (s32[8]{0:T(128)S(1)}, s32[8]{0:T(128)}, u32[]{:S(2)}) copy-start(s32[8]{0:T(128)} %param.28) | copy-start | bytes 100
  75.5 28.5 %copy-start.3 = (bf16[4,2,256,128]{3,2,1,0:T(8,128)(2,1)}, bf16[4,2,256,128]{3,2,1,0:T(8,128)(2,1)S(1)}, u32[]{:S(2)}) copy-start(bf16[4,2,256,128]{3,2,1,0:T(8,128)(2,1)S(1)} %pad_maximum_fusion.2.p0) | copy-start | bytes 1572868
  77.0 20.6 %collective-permute-start.19 = (bf16[4,128,1024]{2,1,0:T(8,128)(2,1)S(1)}, bf16[4,128,1024]{2,1,0:T(8,128)(2,1)}, u32[]{:S(2)}, u32[]{:S(2)}) collective-permute-start(bf16[4,128,1024]{2,1,0:T(8,128)(2,1)S(1)} %slice_bitcast_fusion.1), channel_id=1, source_target_pairs={{0,2},{1,7},{2,4},{3,1},{4,6},{5,3},{6,0},{7,5},{8,10},{9,15},{10,... | collective-permute-start | bytes 3145736 | tf_op jit(solution)/shard_map/ppermute | solution.py:38
  80.0 17.5 %collective-permute-start.26 = (bf16[4,2,256,128]{3,2,1,0:T(8,128)(2,1)S(1)}, bf16[4,2,256,128]{3,2,1,0:T(8,128)(2,1)S(1)}, u32[]{:S(2)}, u32[]{:S(2)}) collective-permute-start(bf16[4,2,256,128]{3,2,1,0:T(8,128)(2,1)S(1)} %pad_maximum_fusion.2.p0), channel_id=1, source_target_pairs={{0,32},{1,9},{2,34},{3,11},{4,36},{5,13},{6,38},{7,15},{8,40},{9,1... | collective-permute-start | bytes 1572872 | tf_op jit(solution)/shard_map/ppermute | solution.py:42
  80.4 17.1 %collective-permute-start.25 = (bf16[4,2,256,128]{3,2,1,0:T(8,128)(2,1)S(1)}, bf16[4,2,256,128]{3,2,1,0:T(8,128)(2,1)S(1)}, u32[]{:S(2)}, u32[]{:S(2)}) collective-permute-start(bf16[4,2,256,128]{3,2,1,0:T(8,128)(2,1)S(1)} %pad_maximum_fusion.2.p0), channel_id=1, source_target_pairs={{0,64},{1,17},{2,66},{3,19},{4,68},{5,21},{6,70},{7,23},{8,72},{9,... | collective-permute-start | bytes 1572872 | tf_op jit(solution)/shard_map/ppermute | solution.py:42
  82.5 15.0 %collective-permute-start.24 = (bf16[4,2,256,128]{3,2,1,0:T(8,128)(2,1)S(1)}, bf16[4,2,256,128]{3,2,1,0:T(8,128)(2,1)S(1)}, u32[]{:S(2)}, u32[]{:S(2)}) collective-permute-start(bf16[4,2,256,128]{3,2,1,0:T(8,128)(2,1)S(1)} %pad_maximum_fusion.2.p0), channel_id=1, source_target_pairs={{0,96},{1,25},{2,98},{3,27},{4,100},{5,29},{6,102},{7,31},{8,104},... | collective-permute-start | bytes 1572872 | tf_op jit(solution)/shard_map/ppermute | solution.py:42
  83.5 1.3 collective-permute-start.20
  84.8 5.6 %collective-permute-start.21 = (f32[8,16,128]{2,1,0:T(8,128)S(1)}, f32[8,16,128]{2,1,0:T(8,128)S(1)}, u32[]{:S(2)}, u32[]{:S(2)}) collective-permute-start(f32[8,16,128]{2,1,0:T(8,128)S(1)} %add.205), channel_id=1, source_target_pairs={{0,6},{1,3},{2,0},{3,5},{4,2},{5,7},{6,4},{7,1},{8,14},{9,11},{10,... | collective-permute-start | bytes 196616 | tf_op jit(solution)/shard_map/ppermute | solution.py:38
  90.4 1.3 collective-permute-start.23
  91.6 4.4 %collective-permute-start.22 = (f32[8,16,128]{2,1,0:T(8,128)S(1)}, f32[8,16,128]{2,1,0:T(8,128)S(1)}, u32[]{:S(2)}, u32[]{:S(2)}) collective-permute-start(f32[8,16,128]{2,1,0:T(8,128)S(1)} %collective-permute-done.21), channel_id=1, source_target_pairs={{0,6},{1,3},{2,0},{3,5},{4,2},{5,7},{6,4},{7,1},{8,14},{9,11},{10,... | collective-permute-start | bytes 196616 | tf_op jit(solution)/shard_map/ppermute | solution.py:38
  96.6 7.3 %collective-permute-start.28 = (bf16[2,4,128,1024]{3,2,1,0:T(8,128)(2,1)}, bf16[2,4,128,1024]{3,2,1,0:T(8,128)(2,1)}, u32[]{:S(2)}, u32[]{:S(2)}) collective-permute-start(bf16[2,4,128,1024]{3,2,1,0:T(8,128)(2,1)} %collective-permute-done.12.near), channel_id=1, source_target_pairs={{0,1},{1,0},{2,3},{3,2},{4,5},{5,4},{6,7},{7,6},{8,9},{9,8},{10,11... | collective-permute-start | bytes 6291464 | tf_op jit(solution)/shard_map/ppermute | solution.py:38
  97.5 6.4 %copy-start.4 = (bf16[4,2,256,128]{3,2,1,0:T(8,128)(2,1)}, bf16[4,2,256,128]{3,2,1,0:T(8,128)(2,1)S(1)}, u32[]{:S(2)}) copy-start(bf16[4,2,256,128]{3,2,1,0:T(8,128)(2,1)S(1)} %collective-permute-done.26.p3) | copy-start | bytes 1572868
  97.6 28.0 %collective-permute-start.27 = (bf16[2,4,128,1024]{3,2,1,0:T(8,128)(2,1)S(1)}, bf16[2,4,128,1024]{3,2,1,0:T(8,128)(2,1)}, u32[]{:S(2)}, u32[]{:S(2)}) collective-permute-start(bf16[2,4,128,1024]{3,2,1,0:T(8,128)(2,1)S(1)} %copy-done.2), channel_id=1, source_target_pairs={{0,2},{1,7},{2,4},{3,1},{4,6},{5,3},{6,0},{7,5},{8,10},{9,15},{10,... | collective-permute-start | bytes 6291464 | tf_op jit(solution)/shard_map/ppermute | solution.py:38
  100.9 3.0 %collective-permute-start.29 = (bf16[4,128,1024]{2,1,0:T(8,128)(2,1)}, bf16[4,128,1024]{2,1,0:T(8,128)(2,1)}, u32[]{:S(2)}, u32[]{:S(2)}) collective-permute-start(bf16[4,128,1024]{2,1,0:T(8,128)(2,1)} %collective-permute-done.19.far), channel_id=1, source_target_pairs={{0,1},{1,0},{2,3},{3,2},{4,5},{5,4},{6,7},{7,6},{8,9},{9,8},{10,11... | collective-permute-start | bytes 3145736 | tf_op jit(solution)/shard_map/ppermute | solution.py:38
  127.9 24.2 %collective-permute-start.31 = (bf16[4,128,1024]{2,1,0:T(8,128)(2,1)}, bf16[4,128,1024]{2,1,0:T(8,128)(2,1)S(1)}, u32[]{:S(2)}, u32[]{:S(2)}) collective-permute-start(bf16[4,128,1024]{2,1,0:T(8,128)(2,1)} %slice_bitcast_fusion), channel_id=1, source_target_pairs={{0,2},{1,7},{2,4},{3,1},{4,6},{5,3},{6,0},{7,5},{8,10},{9,15},{10,... | collective-permute-start | bytes 3145736 | tf_op jit(solution)/shard_map/ppermute | solution.py:38
  130.4 25.8 %collective-permute-start.30 = (bf16[2,4,128,1024]{3,2,1,0:T(8,128)(2,1)}, bf16[2,4,128,1024]{3,2,1,0:T(8,128)(2,1)S(1)}, u32[]{:S(2)}, u32[]{:S(2)}) collective-permute-start(bf16[2,4,128,1024]{3,2,1,0:T(8,128)(2,1)} %collective-permute-done.27.near), channel_id=1, source_target_pairs={{0,1},{1,0},{2,3},{3,2},{4,5},{5,4},{6,7},{7,6},{8,9},{9,8},{10,11... | collective-permute-start | bytes 6291464 | tf_op jit(solution)/shard_map/ppermute | solution.py:38
  152.1 3.1 %collective-permute-start.32 = (bf16[4,128,1024]{2,1,0:T(8,128)(2,1)S(1)}, bf16[4,128,1024]{2,1,0:T(8,128)(2,1)S(1)}, u32[]{:S(2)}, u32[]{:S(2)}) collective-permute-start(bf16[4,128,1024]{2,1,0:T(8,128)(2,1)S(1)} %collective-permute-done.31.far), channel_id=1, source_target_pairs={{0,1},{1,0},{2,3},{3,2},{4,5},{5,4},{6,7},{7,6},{8,9},{9,8},{10,11... | collective-permute-start | bytes 3145736 | tf_op jit(solution)/shard_map/ppermute | solution.py:38
  (9 other events, 21.9 us)

commit v2 on v1

--- a/solution.py
+++ b/solution.py
@@ -16,7 +16,7 @@
 F32 = jnp.float32
 BF16 = jnp.bfloat16
 CHUNKS = (4, 4)
-BLOCKS = ((0, 0, 2), (0, 2, 2), (1, 0, 4))
+BLOCKS = ((0, 0, 4), (1, 0, 4))
 
 SWAP = [(y * 2 + c, y * 2 + 1 - c) for y in range(4) for c in range(2)]
 RING = [(y * 2 + c, (y + 1 - 2 * c) % 4 * 2 + c) for y in range(4) for c in range(2)]
@@ -422,19 +422,17 @@
     low = (chip_low + two_low + one_low + over_tensor(one_low, SWAP)).astype(BF16)
     far = after((over_tensor(near[0], RING),), low, *pairs)[0]
     gathered = [chunks[0], near, over_tensor(near, SWAP), far, over_tensor(far, SWAP)]
-    late_near = over_tensor(after(chunks[1:], far)[0], RING)
+    late_near = over_tensor(after(chunks[1:], one_low, near)[0], RING)
 
     group_1, group_2 = relative(request_group)
     page = request_page_table.reshape(-1) - place * requests
     table = jnp.stack([group_2, group_1, lengths, page], axis=1).astype(jnp.int32)
     tables = rotate_tables(pre, seq)
+    late_far = over_tensor(late_near[0], RING)
+    late_cross = over_tensor(late_near, SWAP)
     outs = ()
     for i, (chunk, start, count) in enumerate(BLOCKS):
         if i == 1:
-            late_near, outs = lax.optimization_barrier((late_near, outs))
-            late_far = over_tensor(late_near[0], RING)
-            late_cross = over_tensor(late_near, SWAP)
-        if i == 2:
             late_far, outs = lax.optimization_barrier((late_far, outs))
             late_far_cross = over_tensor(late_far, SWAP)
             gathered = [chunks[1], late_near, late_cross, late_far, late_far_cross]

time: 191 us -> 202 us (1.058)
  waiting for transfers between devices: 31.7 us -> 51.2 us
  Pallas kernels: 98.1 us -> 87.4 us
    ppermute x12, waiting for transfers between devices: 4.84 us -> 20.2 us  [over_plane(): lax.ppermute(value, ('dp', 'tensor'), plane_shift(k, stage))]
    pallas_call x3 -> x2, Pallas kernels: 76.1 us -> 65.4 us  [block_call(): pl.pallas_call(functools.partial(block_kernel, first, start, count), out_...]
    ppermute x21, waiting for transfers between devices: 26.8 us -> 31 us  [over_tensor(): return lax.ppermute(value, 'tensor', pairs)]
    ppermute x12, starting transfers between devices: 18.3 us -> 14.2 us  [over_plane(): lax.ppermute(value, ('dp', 'tensor'), plane_shift(k, stage))]
    ppermute x21, starting transfers between devices: 24 us -> 27.1 us  [over_tensor(): return lax.ppermute(value, 'tensor', pairs)]
    unnamed x48 -> x44, local copies, waits for them, and re-layouts: 4.18 us -> 5.32 us
  transfers between devices with their start and end apart: 33 -> 33, of which waited for: 13 -> 16; matrix products, arithmetic and copies ran while one was open for 5% -> 7% of each run, Pallas kernels for 34% -> 27%
where the time goes in v2:
time: 202 us; the launch traced here: 201 us
  Pallas kernels  87.4 us (43%)
  waiting for transfers between devices  51.2 us (25%)
  starting transfers between devices  41.3 us (20%)
  other arithmetic  10.1 us (5%)
  local copies, waits for them, and re-layouts  9.97 us (5%)
    pallas_call x2, Pallas kernels, block_call(): pl.pallas_call(functools.partial(block_kernel, first, start, count), out_...  65.4 us
    ppermute x21, waiting for transfers between devices, over_tensor(): return lax.ppermute(value, 'tensor', pairs)  31 us
    ppermute x21, starting transfers between devices, over_tensor(): return lax.ppermute(value, 'tensor', pairs)  27.1 us
    ppermute x12, waiting for transfers between devices, over_plane(): lax.ppermute(value, ('dp', 'tensor'), plane_shift(k, stage))  20.2 us
    ppermute x12, starting transfers between devices, over_plane(): lax.ppermute(value, ('dp', 'tensor'), plane_shift(k, stage))  14.2 us
    pallas_call x2, Pallas kernels, norm_call(): pl.pallas_call(norm_kernel, out_shape=jax.ShapeDtypeStruct((2, count, seq...  9.71 us
    pallas_call x1, Pallas kernels, prefix_call(): pl.pallas_call(prefix_kernel, out_shape=jax.ShapeDtypeStruct((2, rows, HE...  6.36 us
    pallas_call x1, Pallas kernels, low_call(): pl.pallas_call(low_kernel, out_shape=(jax.ShapeDtypeStruct((requests, RAN...  5.97 us
  transfers between devices with their start and end apart: 33, of which 16 were waited for; matrix products, arithmetic and copies ran while one was open for 7% of the time, Pallas kernels for 27%

profile of v2, /device:TPU:1, one launch (start us, length us, event | category | flops | bytes accessed | tf_op | source)
XLA Modules:
  0.0 201.0 jit_solution(877147657886847097)
XLA Ops:
  0.6 1.5 collective-permute-start
  2.2 4.7 %collective-permute-done.12 = bf16[256,1024]{1,0:T(8,128)(2,1)S(1)} collective-permute-done((bf16[256,1024]{1,0:T(8,128)(2,1)}, bf16[256,1024]{1,0:T(8,128)(2,1)S(1)}, u32[]{:S(2)}, u32[]{:S(2)}) %collective-permute-start.12) | collective-permute-done | bytes 524320 | tf_op jit(solution)/shard_map/ppermute | solution.py:38
  6.9 1.1 pad_maximum_fusion.1.mine
  8.0 2.9 %collective-permute-start.13 = (bf16[2,256,1024]{2,1,0:T(8,128)(2,1)S(1)}, bf16[2,256,1024]{2,1,0:T(8,128)(2,1)S(1)}, u32[]{:S(2)}, u32[]{:S(2)}) collective-permute-start(bf16[2,256,1024]{2,1,0:T(8,128)(2,1)S(1)} %pad_maximum_fusion.1.mine), channel_id=1, source_target_pairs={{0,2},{1,7},{2,4},{3,1},{4,6},{5,3},{6,0},{7,5},{8,10},{9,15},{10,... | collective-permute-start | bytes 3145736 | tf_op jit(solution)/shard_map/ppermute | solution.py:38
  10.9 1.0 pad_maximum_fusion.3
  11.9 3.8 %collective-permute-start.2 = (bf16[4,32,1024]{2,1,0:T(8,128)(2,1)S(1)}, bf16[4,32,1024]{2,1,0:T(8,128)(2,1)S(1)}, u32[]{:S(2)}, u32[]{:S(2)}) collective-permute-start(bf16[4,32,1024]{2,1,0:T(8,128)(2,1)S(1)} %pad_maximum_fusion.3), channel_id=1, source_target_pairs={{0,24},{1,97},{2,26},{3,99},{4,28},{5,101},{6,30},{7,103},{8,0},{9... | collective-permute-start | bytes 786440 | tf_op jit(solution)/shard_map/ppermute | solution.py:42
  17.5 4.4 %collective-permute-done.2 = bf16[4,32,1024]{2,1,0:T(8,128)(2,1)S(1)} collective-permute-done((bf16[4,32,1024]{2,1,0:T(8,128)(2,1)S(1)}, bf16[4,32,1024]{2,1,0:T(8,128)(2,1)S(1)}, u32[]{:S(2)}, u32[]{:S(2)}) %collective-permute-start.2) | collective-permute-done | bytes 262176 | tf_op jit(solution)/shard_map/ppermute | solution.py:42
  22.6 2.4 %collective-permute-done.4 = bf16[4,32,1024]{2,1,0:T(8,128)(2,1)S(1)} collective-permute-done((bf16[4,32,1024]{2,1,0:T(8,128)(2,1)S(1)}, bf16[4,32,1024]{2,1,0:T(8,128)(2,1)S(1)}, u32[]{:S(2)}, u32[]{:S(2)}) %collective-permute-start.4) | collective-permute-done | bytes 262176 | tf_op jit(solution)/shard_map/ppermute | solution.py:42
  25.0 1.1 pad_maximum_fusion.a0
  26.1 2.5 %collective-permute-start.7 = (bf16[4,4,32,1024]{3,2,1,0:T(8,128)(2,1)}, bf16[4,4,32,1024]{3,2,1,0:T(8,128)(2,1)S(1)}, u32[]{:S(2)}, u32[]{:S(2)}) collective-permute-start(bf16[4,4,32,1024]{3,2,1,0:T(8,128)(2,1)} %pad_maximum_fusion.a0), channel_id=1, source_target_pairs={{0,96},{1,25},{2,98},{3,27},{4,100},{5,29},{6,102},{7,31},{8,104},... | collective-permute-start | bytes 3145736 | tf_op jit(solution)/shard_map/ppermute | solution.py:42
  28.6 3.7 %collective-permute-done.1 = f32[8,128]{1,0:T(8,128)S(1)} collective-permute-done((f32[8,128]{1,0:T(8,128)S(1)}, f32[8,128]{1,0:T(8,128)S(1)}, u32[]{:S(2)}, u32[]{:S(2)}) %collective-permute-start.1) | collective-permute-done | bytes 4128 | tf_op jit(solution)/shard_map/ppermute | solution.py:38
  32.3 4.1 %collective-permute-start.6 = (f32[8,128]{1,0:T(8,128)S(1)}, f32[8,128]{1,0:T(8,128)S(1)}, u32[]{:S(2)}, u32[]{:S(2)}) collective-permute-start(f32[8,128]{1,0:T(8,128)S(1)} %collective-permute-done.1), channel_id=1, source_target_pairs={{0,1},{1,0},{2,3},{3,2},{4,5},{5,4},{6,7},{7,6},{8,9},{9,8},{10,11... | collective-permute-start | bytes 12296 | tf_op jit(solution)/shard_map/ppermute | solution.py:38
  37.8 1.0 copy-done.5
  40.3 4.9 %norm.3.x0.mine = bf16[2,4,128,1024]{3,2,1,0:T(8,128)(2,1)} custom-call(s32[2]{0:T(128)} %pad_add_fusion.2.place, bf16[8,128,1024]{2,1,0:T(8,128)(2,1)} %own.3, bf16[8,128,1024]{2,1,0:T(8,128)(2,1)} %copy-done.1, f32[8,1,128]{2,1,0:T(1,128)} %bitcast.48, f32[8,1,1024]{2,1,0:T(1,128)} %bitcast.33, f32[8,1,1024]{2,1,0:T(1,128)} %bitcast.34), custom_call_target="tpu_custom_call" | custom-call | tf_op jit(solution)/shard_map/norm/pallas_call | solution.py:79
  45.2 2.1 %collective-permute-done.14.far = bf16[256,1024]{1,0:T(8,128)(2,1)} collective-permute-done((bf16[256,1024]{1,0:T(8,128)(2,1)S(1)}, bf16[256,1024]{1,0:T(8,128)(2,1)}, u32[]{:S(2)}, u32[]{:S(2)}) %collective-permute-start.14) | collective-permute-done | bytes 524320 | tf_op jit(solution)/shard_map/ppermute | solution.py:38
  47.3 1.0 copy-done.13
  48.3 1.2 collective-permute-start.15
  49.5 1.7 collective-permute-start.16
  51.7 1.4 collective-permute-start.17
  54.0 0.9 collective-permute-done.17.far_cross
  55.0 6.4 %prefix.1 = bf16[2,256,128]{2,1,0:T(8,128)(2,1)} custom-call(s32[8]{0:T(128)} %stack.92.order, bf16[2,256,1024]{2,1,0:T(8,128)(2,1)} %copy-done.4, bf16[2,256,1024]{2,1,0:T(8,128)(2,1)} %copy-done.5, bf16[2,256,1024]{2,1,0:T(8,128)(2,1)} %copy-done.11, bf16[256,1024]{1,0:T(8,128)(2,1)} %collective-permute-done.14.far, ...), custom_call_target="tpu_custom_call" | custom-call | tf_op jit(solution)/shard_map/prefix/pallas_call | solution.py:120
  61.3 2.5 %collective-permute-start.18 = (bf16[2,256,128]{2,1,0:T(8,128)(2,1)}, bf16[2,256,128]{2,1,0:T(8,128)(2,1)S(1)}, u32[]{:S(2)}, u32[]{:S(2)}) collective-permute-start(bf16[2,256,128]{2,1,0:T(8,128)(2,1)} %prefix.1), channel_id=1, source_target_pairs={{0,24},{1,97},{2,26},{3,99},{4,28},{5,101},{6,30},{7,103},{8,0},{9... | collective-permute-start | bytes 393224 | tf_op jit(solution)/shard_map/ppermute | solution.py:42
  63.8 1.2 collective-permute-start.19
  65.8 4.8 %norm.2.x1.mine = bf16[2,4,128,1024]{3,2,1,0:T(8,128)(2,1)} custom-call(s32[2]{0:T(128)} %pad_add_fusion.2.place, bf16[8,128,1024]{2,1,0:T(8,128)(2,1)} %own.3, bf16[8,128,1024]{2,1,0:T(8,128)(2,1)} %copy-done.1, f32[8,1,128]{2,1,0:T(1,128)} %bitcast.49, f32[8,1,1024]{2,1,0:T(1,128)} %bitcast.36, f32[8,1,1024]{2,1,0:T(1,128)} %bitcast.37), custom_call_target="tpu_custom_call" | custom-call | tf_op jit(solution)/shard_map/norm/pallas_call | solution.py:79
  70.6 1.0 copy-done.14
  71.5 6.0 %low.1 = (f32[8,16,128]{2,1,0:T(8,128)}, bf16[8,16,1024]{2,1,0:T(8,128)(2,1)}) custom-call(s32[8,3]{1,0:T(8,128)} %pad_add_fusion.1.pick, bf16[2,4,128,1024]{3,2,1,0:T(8,128)(2,1)} %norm.3.x0.mine, bf16[2,4,128,1024]{3,2,1,0:T(8,128)(2,1)} %norm.2.x1.mine, bf16[4,4,32,1024]{3,2,1,0:T(8,128)(2,1)} %pad_maximum_fusion.a0, bf16[4,4,32,1024]{3,2,1,0:T(8,128)(2,1)} %copy-done.13, ...), custom_call_target="tpu_custom_call" | custom-call | tf_op jit(solution)/shard_map/low/pallas_call | solution.py:156
  77.6 1.5 collective-permute-done.10
  79.1 0.8 add.205
  80.7 1.0 pad_maximum_fusion.2.p0
  81.7 3.0 %collective-permute-done.11 = f32[8,16,128]{2,1,0:T(8,128)S(1)} collective-permute-done((f32[8,16,128]{2,1,0:T(8,128)S(1)}, f32[8,16,128]{2,1,0:T(8,128)S(1)}, u32[]{:S(2)}, u32[]{:S(2)}) %collective-permute-start.11) | collective-permute-done | bytes 65568 | tf_op jit(solution)/shard_map/ppermute | solution.py:38
  84.7 1.5 collective-permute-start.21
  86.9 1.3 slice_bitcast_fusion.1
  88.8 3.5 %collective-permute-start.24 = (bf16[2,4,128,1024]{3,2,1,0:T(8,128)(2,1)}, bf16[2,4,128,1024]{3,2,1,0:T(8,128)(2,1)}, u32[]{:S(2)}, u32[]{:S(2)}) collective-permute-start(bf16[2,4,128,1024]{3,2,1,0:T(8,128)(2,1)} %collective-permute-done.15.near), channel_id=1, source_target_pairs={{0,1},{1,0},{2,3},{3,2},{4,5},{5,4},{6,7},{7,6},{8,9},{9,8},{10,11... | collective-permute-start | bytes 6291464 | tf_op jit(solution)/shard_map/ppermute | solution.py:38
  92.3 2.1 %collective-permute-start.26 = (f32[8,16,128]{2,1,0:T(8,128)S(1)}, f32[8,16,128]{2,1,0:T(8,128)S(1)}, u32[]{:S(2)}, u32[]{:S(2)}) collective-permute-start(f32[8,16,128]{2,1,0:T(8,128)S(1)} %collective-permute-done.11), channel_id=1, source_target_pairs={{0,6},{1,3},{2,0},{3,5},{4,2},{5,7},{6,4},{7,1},{8,14},{9,11},{10,... | collective-permute-start | bytes 196616 | tf_op jit(solution)/shard_map/ppermute | solution.py:38
  94.5 3.3 %collective-permute-done.26 = f32[8,16,128]{2,1,0:T(8,128)S(1)} collective-permute-done((f32[8,16,128]{2,1,0:T(8,128)S(1)}, f32[8,16,128]{2,1,0:T(8,128)S(1)}, u32[]{:S(2)}, u32[]{:S(2)}) %collective-permute-start.26) | collective-permute-done | bytes 65568 | tf_op jit(solution)/shard_map/ppermute | solution.py:38
  97.8 1.3 collective-permute-done.27
  99.1 2.2 %collective-permute-start.29 = (bf16[4,2,256,128]{3,2,1,0:T(8,128)(2,1)S(1)}, bf16[4,2,256,128]{3,2,1,0:T(8,128)(2,1)S(1)}, u32[]{:S(2)}, u32[]{:S(2)}) collective-permute-start(bf16[4,2,256,128]{3,2,1,0:T(8,128)(2,1)S(1)} %pad_maximum_fusion.2.p0), channel_id=1, source_target_pairs={{0,64},{1,17},{2,66},{3,19},{4,68},{5,21},{6,70},{7,23},{8,72},{9,... | collective-permute-start | bytes 1572872 | tf_op jit(solution)/shard_map/ppermute | solution.py:42
  102.0 7.0 %collective-permute-done.29.p2 = bf16[4,2,256,128]{3,2,1,0:T(8,128)(2,1)S(1)} collective-permute-done((bf16[4,2,256,128]{3,2,1,0:T(8,128)(2,1)S(1)}, bf16[4,2,256,128]{3,2,1,0:T(8,128)(2,1)S(1)}, u32[]{:S(2)}, u32[]{:S(2)}) %collective-permute-start.29) | collective-permute-done | bytes 524320 | tf_op jit(solution)/shard_map/ppermute | solution.py:42
  109.0 5.7 %collective-permute-done.30.p3 = bf16[4,2,256,128]{3,2,1,0:T(8,128)(2,1)S(1)} collective-permute-done((bf16[4,2,256,128]{3,2,1,0:T(8,128)(2,1)S(1)}, bf16[4,2,256,128]{3,2,1,0:T(8,128)(2,1)S(1)}, u32[]{:S(2)}, u32[]{:S(2)}) %collective-permute-start.30) | collective-permute-done | bytes 524320 | tf_op jit(solution)/shard_map/ppermute | solution.py:42
  114.6 7.3 %collective-permute-done.25.far = bf16[4,128,1024]{2,1,0:T(8,128)(2,1)} collective-permute-done((bf16[4,128,1024]{2,1,0:T(8,128)(2,1)S(1)}, bf16[4,128,1024]{2,1,0:T(8,128)(2,1)}, u32[]{:S(2)}, u32[]{:S(2)}) %collective-permute-start.25) | collective-permute-done | bytes 1048608 | tf_op jit(solution)/shard_map/ppermute | solution.py:38
  121.9 3.1 %collective-permute-start.31 = (bf16[4,128,1024]{2,1,0:T(8,128)(2,1)}, bf16[4,128,1024]{2,1,0:T(8,128)(2,1)}, u32[]{:S(2)}, u32[]{:S(2)}) collective-permute-start(bf16[4,128,1024]{2,1,0:T(8,128)(2,1)} %collective-permute-done.25.far), channel_id=1, source_target_pairs={{0,1},{1,0},{2,3},{3,2},{4,5},{5,4},{6,7},{7,6},{8,9},{9,8},{10,11... | collective-permute-start | bytes 3145736 | tf_op jit(solution)/shard_map/ppermute | solution.py:38
  125.0 2.3 %slice_bitcast_fusion = bf16[4,128,1024]{2,1,0:T(8,128)(2,1)} fusion(bf16[2,4,128,1024]{3,2,1,0:T(8,128)(2,1)} %collective-permute-done.21.near), kind=kLoop, calls=%fused_computation.2 | loop fusion | bytes 2097152 | tf_op jit(solution)/shard_map/squeeze | solution.py:431
  127.3 1.7 collective-permute-start.23
  130.1 32.7 %block.2 = (bf16[8,128,1024]{2,1,0:T(8,128)(2,1)}, bf16[8,2,128,128]{3,2,1,0:T(8,128)(2,1)}) custom-call(s32[8]{0:T(128)} %stack.92.order, s32[8,4]{1,0:T(8,128)} %pad_add_fusion.table, bf16[2,4,128,1024]{3,2,1,0:T(8,128)(2,1)} %norm.3.x0.mine, bf16[2,4,128,1024]{3,2,1,0:T(8,128)(2,1)} %collective-permute-done.15.near, ...), custom_call_target="tpu_custom_call" | custom-call | tf_op jit(solution)/shard_map/block/pallas_call | solution.py:298
  163.4 2.5 %collective-permute-done.32.far_cross = bf16[4,128,1024]{2,1,0:T(8,128)(2,1)S(1)} collective-permute-done((bf16[4,128,1024]{2,1,0:T(8,128)(2,1)}, bf16[4,128,1024]{2,1,0:T(8,128)(2,1)S(1)}, u32[]{:S(2)}, u32[]{:S(2)}) %collective-permute-start.32) | collective-permute-done | bytes 1048608 | tf_op jit(solution)/shard_map/ppermute | solution.py:38
  165.9 1.0 copy-done.12
  166.8 1.3 copy-done.10
  168.2 32.7 %block.3 = (bf16[8,128,1024]{2,1,0:T(8,128)(2,1)}, bf16[8,2,128,128]{3,2,1,0:T(8,128)(2,1)}) custom-call(s32[8]{0:T(128)} %stack.92.order, s32[8,4]{1,0:T(8,128)} %pad_add_fusion.table, bf16[2,4,128,1024]{3,2,1,0:T(8,128)(2,1)} %norm.2.x1.mine, ...), custom_call_target="tpu_custom_call", output_to_operand_aliasing={{0}: (18, {}), {1}: (19, {})} | custom-call | tf_op jit(solution)/shard_map/block/pallas_call | solution.py:298
  (96 shorter events, 12.2 us)
Async XLA Ops:
  0.6 15.8 %copy-start = (bf16[8,128,1024]{2,1,0:T(8,128)(2,1)S(1)}, bf16[8,128,1024]{2,1,0:T(8,128)(2,1)}, u32[]{:S(2)}) copy-start(bf16[8,128,1024]{2,1,0:T(8,128)(2,1)} %own.3) | copy-start | bytes 6291460
  0.6 16.3 %collective-permute-start = (bf16[8,128,1024]{2,1,0:T(8,128)(2,1)}, bf16[8,128,1024]{2,1,0:T(8,128)(2,1)S(1)}, u32[]{:S(2)}, u32[]{:S(2)}) collective-permute-start(bf16[8,128,1024]{2,1,0:T(8,128)(2,1)} %own.3), channel_id=1, source_target_pairs={{0,1},{1,0},{2,3},{3,2},{4,5},{5,4},{6,7},{7,6},{8,9},{9,8},{10,11... | collective-permute-start | bytes 6291464 | tf_op jit(solution)/shard_map/ppermute | solution.py:38
  2.1 4.7 %collective-permute-start.12 = (bf16[256,1024]{1,0:T(8,128)(2,1)}, bf16[256,1024]{1,0:T(8,128)(2,1)S(1)}, u32[]{:S(2)}, u32[]{:S(2)}) collective-permute-start(bf16[256,1024]{1,0:T(8,128)(2,1)} %bitcast.40), channel_id=1, source_target_pairs={{0,1},{1,0},{2,3},{3,2},{4,5},{5,4},{6,7},{7,6},{8,9},{9,8},{10,11... | collective-permute-start | bytes 1572872 | tf_op jit(solution)/shard_map/ppermute | solution.py:38
  8.0 9.4 %copy-start.4 = (bf16[2,256,1024]{2,1,0:T(8,128)(2,1)}, bf16[2,256,1024]{2,1,0:T(8,128)(2,1)S(1)}, u32[]{:S(2)}) copy-start(bf16[2,256,1024]{2,1,0:T(8,128)(2,1)S(1)} %pad_maximum_fusion.1.mine) | copy-start | bytes 3145732
  8.0 29.7 %collective-permute-start.13 = (bf16[2,256,1024]{2,1,0:T(8,128)(2,1)S(1)}, bf16[2,256,1024]{2,1,0:T(8,128)(2,1)S(1)}, u32[]{:S(2)}, u32[]{:S(2)}) collective-permute-start(bf16[2,256,1024]{2,1,0:T(8,128)(2,1)S(1)} %pad_maximum_fusion.1.mine), channel_id=1, source_target_pairs={{0,2},{1,7},{2,4},{3,1},{4,6},{5,3},{6,0},{7,5},{8,10},{9,15},{10,... | collective-permute-start | bytes 3145736 | tf_op jit(solution)/shard_map/ppermute | solution.py:38
  11.9 10.0 %collective-permute-start.2 = (bf16[4,32,1024]{2,1,0:T(8,128)(2,1)S(1)}, bf16[4,32,1024]{2,1,0:T(8,128)(2,1)S(1)}, u32[]{:S(2)}, u32[]{:S(2)}) collective-permute-start(bf16[4,32,1024]{2,1,0:T(8,128)(2,1)S(1)} %pad_maximum_fusion.3), channel_id=1, source_target_pairs={{0,24},{1,97},{2,26},{3,99},{4,28},{5,101},{6,30},{7,103},{8,0},{9... | collective-permute-start | bytes 786440 | tf_op jit(solution)/shard_map/ppermute | solution.py:42
  15.7 6.8 %collective-permute-start.3 = (bf16[4,32,1024]{2,1,0:T(8,128)(2,1)S(1)}, bf16[4,32,1024]{2,1,0:T(8,128)(2,1)S(1)}, u32[]{:S(2)}, u32[]{:S(2)}) collective-permute-start(bf16[4,32,1024]{2,1,0:T(8,128)(2,1)S(1)} %pad_maximum_fusion.3), channel_id=1, source_target_pairs={{0,16},{1,65},{2,18},{3,67},{4,20},{5,69},{6,22},{7,71},{8,24},{9,... | collective-permute-start | bytes 786440 | tf_op jit(solution)/shard_map/ppermute | solution.py:42
  15.7 9.2 %collective-permute-start.4 = (bf16[4,32,1024]{2,1,0:T(8,128)(2,1)S(1)}, bf16[4,32,1024]{2,1,0:T(8,128)(2,1)S(1)}, u32[]{:S(2)}, u32[]{:S(2)}) collective-permute-start(bf16[4,32,1024]{2,1,0:T(8,128)(2,1)S(1)} %pad_maximum_fusion.3), channel_id=1, source_target_pairs={{0,8},{1,33},{2,10},{3,35},{4,12},{5,37},{6,14},{7,39},{8,16},{9,4... | collective-permute-start | bytes 786440 | tf_op jit(solution)/shard_map/ppermute | solution.py:42
  16.9 9.2 %copy-start.1 = (bf16[8,128,1024]{2,1,0:T(8,128)(2,1)}, bf16[8,128,1024]{2,1,0:T(8,128)(2,1)S(1)}, u32[]{:S(2)}) copy-start(bf16[8,128,1024]{2,1,0:T(8,128)(2,1)S(1)} %collective-permute-done.other) | copy-start | bytes 6291460
  17.4 21.7 %copy-start.16 = (bf16[8192]{0:T(1024)(128)(2,1)S(1)}, bf16[8192]{0:T(1024)(128)(2,1)}, u32[]{:S(2)}) copy-start(bf16[8192]{0:T(1024)(128)(2,1)} %param.19) | copy-start | bytes 49156
  26.1 21.2 %collective-permute-start.7 = (bf16[4,4,32,1024]{3,2,1,0:T(8,128)(2,1)}, bf16[4,4,32,1024]{3,2,1,0:T(8,128)(2,1)S(1)}, u32[]{:S(2)}, u32[]{:S(2)}) collective-permute-start(bf16[4,4,32,1024]{3,2,1,0:T(8,128)(2,1)} %pad_maximum_fusion.a0), channel_id=1, source_target_pairs={{0,96},{1,25},{2,98},{3,27},{4,100},{5,29},{6,102},{7,31},{8,104},... | collective-permute-start | bytes 3145736 | tf_op jit(solution)/shard_map/ppermute | solution.py:42
  28.6 18.7 %collective-permute-start.9 = (bf16[4,4,32,1024]{3,2,1,0:T(8,128)(2,1)}, bf16[4,4,32,1024]{3,2,1,0:T(8,128)(2,1)}, u32[]{:S(2)}, u32[]{:S(2)}) collective-permute-start(bf16[4,4,32,1024]{3,2,1,0:T(8,128)(2,1)} %pad_maximum_fusion.a0), channel_id=1, source_target_pairs={{0,32},{1,9},{2,34},{3,11},{4,36},{5,13},{6,38},{7,15},{8,40},{9,1... | collective-permute-start | bytes 3145736 | tf_op jit(solution)/shard_map/ppermute | solution.py:42
  28.6 3.7 %collective-permute-start.1 = (f32[8,128]{1,0:T(8,128)S(1)}, f32[8,128]{1,0:T(8,128)S(1)}, u32[]{:S(2)}, u32[]{:S(2)}) collective-permute-start(f32[8,128]{1,0:T(8,128)S(1)} %add.195), channel_id=1, source_target_pairs={{0,6},{1,3},{2,0},{3,5},{4,2},{5,7},{6,4},{7,1},{8,14},{9,11},{10,... | collective-permute-start | bytes 12296 | tf_op jit(solution)/shard_map/ppermute | solution.py:38
  32.3 4.1 %collective-permute-start.5 = (f32[8,128]{1,0:T(8,128)S(1)}, f32[8,128]{1,0:T(8,128)S(1)}, u32[]{:S(2)}, u32[]{:S(2)}) collective-permute-start(f32[8,128]{1,0:T(8,128)S(1)} %collective-permute-done.1), channel_id=1, source_target_pairs={{0,6},{1,3},{2,0},{3,5},{4,2},{5,7},{6,4},{7,1},{8,14},{9,11},{10,... | collective-permute-start | bytes 12296 | tf_op jit(solution)/shard_map/ppermute | solution.py:38
  32.3 4.9 %collective-permute-start.6 = (f32[8,128]{1,0:T(8,128)S(1)}, f32[8,128]{1,0:T(8,128)S(1)}, u32[]{:S(2)}, u32[]{:S(2)}) collective-permute-start(f32[8,128]{1,0:T(8,128)S(1)} %collective-permute-done.1), channel_id=1, source_target_pairs={{0,1},{1,0},{2,3},{3,2},{4,5},{5,4},{6,7},{7,6},{8,9},{9,8},{10,11... | collective-permute-start | bytes 12296 | tf_op jit(solution)/shard_map/ppermute | solution.py:38
  38.8 8.5 %collective-permute-start.14 = (bf16[256,1024]{1,0:T(8,128)(2,1)S(1)}, bf16[256,1024]{1,0:T(8,128)(2,1)}, u32[]{:S(2)}, u32[]{:S(2)}) collective-permute-start(bf16[256,1024]{1,0:T(8,128)(2,1)S(1)} %slice_bitcast_fusion.2), channel_id=1, source_target_pairs={{0,2},{1,7},{2,4},{3,1},{4,6},{5,3},{6,0},{7,5},{8,10},{9,15},{10,... | collective-permute-start | bytes 1572872 | tf_op jit(solution)/shard_map/ppermute | solution.py:38
  40.3 9.1 %copy-start.6 = (bf16[2,256,1024]{2,1,0:T(8,128)(2,1)S(1)}, bf16[2,256,1024]{2,1,0:T(8,128)(2,1)}, u32[]{:S(2)}) copy-start(bf16[2,256,1024]{2,1,0:T(8,128)(2,1)} %copy-done.5) | copy-start | bytes 3145732
  40.3 12.8 %copy-start.19 = (s32[64]{0:T(128)S(1)}, s32[64]{0:T(128)}, u32[]{:S(2)}) copy-start(s32[64]{0:T(128)} %param.25) | copy-start | bytes 772
  40.3 12.8 %copy-start.20 = (s32[8]{0:T(128)S(1)}, s32[8]{0:T(128)}, u32[]{:S(2)}) copy-start(s32[8]{0:T(128)} %param.26) | copy-start | bytes 100
  48.3 33.4 %collective-permute-start.15 = (bf16[2,4,128,1024]{3,2,1,0:T(8,128)(2,1)}, bf16[2,4,128,1024]{3,2,1,0:T(8,128)(2,1)}, u32[]{:S(2)}, u32[]{:S(2)}) collective-permute-start(bf16[2,4,128,1024]{3,2,1,0:T(8,128)(2,1)} %norm.3.x0.mine), channel_id=1, source_target_pairs={{0,2},{1,7},{2,4},{3,1},{4,6},{5,3},{6,0},{7,5},{8,10},{9,15},{10,... | collective-permute-start | bytes 6291464 | tf_op jit(solution)/shard_map/ppermute | solution.py:38
  49.5 4.6 %collective-permute-start.16 = (bf16[2,256,1024]{2,1,0:T(8,128)(2,1)S(1)}, bf16[2,256,1024]{2,1,0:T(8,128)(2,1)S(1)}, u32[]{:S(2)}, u32[]{:S(2)}) collective-permute-start(bf16[2,256,1024]{2,1,0:T(8,128)(2,1)S(1)} %copy-done.6), channel_id=1, source_target_pairs={{0,1},{1,0},{2,3},{3,2},{4,5},{5,4},{6,7},{7,6},{8,9},{9,8},{10,11... | collective-permute-start | bytes 3145736 | tf_op jit(solution)/shard_map/ppermute | solution.py:38
  51.1 19.4 %collective-permute-start.8 = (bf16[4,4,32,1024]{3,2,1,0:T(8,128)(2,1)}, bf16[4,4,32,1024]{3,2,1,0:T(8,128)(2,1)S(1)}, u32[]{:S(2)}, u32[]{:S(2)}) collective-permute-start(bf16[4,4,32,1024]{3,2,1,0:T(8,128)(2,1)} %pad_maximum_fusion.a0), channel_id=1, source_target_pairs={{0,64},{1,17},{2,66},{3,19},{4,68},{5,21},{6,70},{7,23},{8,72},{9,... | collective-permute-start | bytes 3145736 | tf_op jit(solution)/shard_map/ppermute | solution.py:42
  51.7 3.3 %collective-permute-start.17 = (bf16[256,1024]{1,0:T(8,128)(2,1)}, bf16[256,1024]{1,0:T(8,128)(2,1)}, u32[]{:S(2)}, u32[]{:S(2)}) collective-permute-start(bf16[256,1024]{1,0:T(8,128)(2,1)} %collective-permute-done.14.far), channel_id=1, source_target_pairs={{0,1},{1,0},{2,3},{3,2},{4,5},{5,4},{6,7},{7,6},{8,9},{9,8},{10,11... | collective-permute-start | bytes 1572872 | tf_op jit(solution)/shard_map/ppermute | solution.py:38
  61.3 19.3 %collective-permute-start.18 = (bf16[2,256,128]{2,1,0:T(8,128)(2,1)}, bf16[2,256,128]{2,1,0:T(8,128)(2,1)S(1)}, u32[]{:S(2)}, u32[]{:S(2)}) collective-permute-start(bf16[2,256,128]{2,1,0:T(8,128)(2,1)} %prefix.1), channel_id=1, source_target_pairs={{0,24},{1,97},{2,26},{3,99},{4,28},{5,101},{6,30},{7,103},{8,0},{9... | collective-permute-start | bytes 393224 | tf_op jit(solution)/shard_map/ppermute | solution.py:42
  63.8 16.8 %collective-permute-start.19 = (bf16[2,256,128]{2,1,0:T(8,128)(2,1)}, bf16[2,256,128]{2,1,0:T(8,128)(2,1)S(1)}, u32[]{:S(2)}, u32[]{:S(2)}) collective-permute-start(bf16[2,256,128]{2,1,0:T(8,128)(2,1)} %prefix.1), channel_id=1, source_target_pairs={{0,16},{1,65},{2,18},{3,67},{4,20},{5,69},{6,22},{7,71},{8,24},{9,... | collective-permute-start | bytes 393224 | tf_op jit(solution)/shard_map/ppermute | solution.py:42
  65.1 15.6 %collective-permute-start.20 = (bf16[2,256,128]{2,1,0:T(8,128)(2,1)}, bf16[2,256,128]{2,1,0:T(8,128)(2,1)}, u32[]{:S(2)}, u32[]{:S(2)}) collective-permute-start(bf16[2,256,128]{2,1,0:T(8,128)(2,1)} %prefix.1), channel_id=1, source_target_pairs={{0,8},{1,33},{2,10},{3,35},{4,12},{5,37},{6,14},{7,39},{8,16},{9,4... | collective-permute-start | bytes 393224 | tf_op jit(solution)/shard_map/ppermute | solution.py:42
  70.6 10.1 %copy-start.15 = (bf16[2,256,128]{2,1,0:T(8,128)(2,1)S(1)}, bf16[2,256,128]{2,1,0:T(8,128)(2,1)}, u32[]{:S(2)}) copy-start(bf16[2,256,128]{2,1,0:T(8,128)(2,1)} %prefix.1) | copy-start | bytes 393220
  70.6 14.1 %copy-start.2 = (bf16[2,4,128,1024]{3,2,1,0:T(8,128)(2,1)S(1)}, bf16[2,4,128,1024]{3,2,1,0:T(8,128)(2,1)}, u32[]{:S(2)}) copy-start(bf16[2,4,128,1024]{3,2,1,0:T(8,128)(2,1)} %norm.2.x1.mine) | copy-start | bytes 6291460
  77.5 1.5 collective-permute-start.10
  79.9 4.8 %collective-permute-start.11 = (f32[8,16,128]{2,1,0:T(8,128)S(1)}, f32[8,16,128]{2,1,0:T(8,128)S(1)}, u32[]{:S(2)}, u32[]{:S(2)}) collective-permute-start(f32[8,16,128]{2,1,0:T(8,128)S(1)} %add.205), channel_id=1, source_target_pairs={{0,6},{1,3},{2,0},{3,5},{4,2},{5,7},{6,4},{7,1},{8,14},{9,11},{10,... | collective-permute-start | bytes 196616 | tf_op jit(solution)/shard_map/ppermute | solution.py:38
  81.6 45.6 %copy-start.3 = (bf16[4,2,256,128]{3,2,1,0:T(8,128)(2,1)}, bf16[4,2,256,128]{3,2,1,0:T(8,128)(2,1)S(1)}, u32[]{:S(2)}) copy-start(bf16[4,2,256,128]{3,2,1,0:T(8,128)(2,1)S(1)} %pad_maximum_fusion.2.p0) | copy-start | bytes 1572868
  81.7 47.4 %copy-start.17 = (s32[8]{0:T(128)S(1)}, s32[8]{0:T(128)}, u32[]{:S(2)}) copy-start(s32[8]{0:T(128)} %param.27) | copy-start | bytes 100
  81.7 47.6 %copy-start.21 = (s32[8,1]{0,1:T(1,128)S(1)}, s32[8,1]{0,1:T(1,128)}, u32[]{:S(2)}) copy-start(s32[8,1]{0,1:T(1,128)} %param.29) | copy-start | bytes 100
  81.7 47.6 %copy-start.18 = (s32[8]{0:T(128)S(1)}, s32[8]{0:T(128)}, u32[]{:S(2)}) copy-start(s32[8]{0:T(128)} %param.28) | copy-start | bytes 100
  84.7 40.3 %collective-permute-start.21 = (bf16[2,4,128,1024]{3,2,1,0:T(8,128)(2,1)S(1)}, bf16[2,4,128,1024]{3,2,1,0:T(8,128)(2,1)}, u32[]{:S(2)}, u32[]{:S(2)}) collective-permute-start(bf16[2,4,128,1024]{3,2,1,0:T(8,128)(2,1)S(1)} %copy-done.2), channel_id=1, source_target_pairs={{0,2},{1,7},{2,4},{3,1},{4,6},{5,3},{6,0},{7,5},{8,10},{9,15},{10,... | collective-permute-start | bytes 6291464 | tf_op jit(solution)/shard_map/ppermute | solution.py:38
  86.2 15.1 %collective-permute-start.28 = (bf16[4,2,256,128]{3,2,1,0:T(8,128)(2,1)S(1)}, bf16[4,2,256,128]{3,2,1,0:T(8,128)(2,1)S(1)}, u32[]{:S(2)}, u32[]{:S(2)}) collective-permute-start(bf16[4,2,256,128]{3,2,1,0:T(8,128)(2,1)S(1)} %pad_maximum_fusion.2.p0), channel_id=1, source_target_pairs={{0,96},{1,25},{2,98},{3,27},{4,100},{5,29},{6,102},{7,31},{8,104},... | collective-permute-start | bytes 1572872 | tf_op jit(solution)/shard_map/ppermute | solution.py:42
  88.2 33.7 %collective-permute-start.25 = (bf16[4,128,1024]{2,1,0:T(8,128)(2,1)S(1)}, bf16[4,128,1024]{2,1,0:T(8,128)(2,1)}, u32[]{:S(2)}, u32[]{:S(2)}) collective-permute-start(bf16[4,128,1024]{2,1,0:T(8,128)(2,1)S(1)} %slice_bitcast_fusion.1), channel_id=1, source_target_pairs={{0,2},{1,7},{2,4},{3,1},{4,6},{5,3},{6,0},{7,5},{8,10},{9,15},{10,... | collective-permute-start | bytes 3145736 | tf_op jit(solution)/shard_map/ppermute | solution.py:38
  88.8 41.3 %collective-permute-start.24 = (bf16[2,4,128,1024]{3,2,1,0:T(8,128)(2,1)}, bf16[2,4,128,1024]{3,2,1,0:T(8,128)(2,1)}, u32[]{:S(2)}, u32[]{:S(2)}) collective-permute-start(bf16[2,4,128,1024]{3,2,1,0:T(8,128)(2,1)} %collective-permute-done.15.near), channel_id=1, source_target_pairs={{0,1},{1,0},{2,3},{3,2},{4,5},{5,4},{6,7},{7,6},{8,9},{9,8},{10,11... | collective-permute-start | bytes 6291464 | tf_op jit(solution)/shard_map/ppermute | solution.py:38
  92.3 5.5 %collective-permute-start.26 = (f32[8,16,128]{2,1,0:T(8,128)S(1)}, f32[8,16,128]{2,1,0:T(8,128)S(1)}, u32[]{:S(2)}, u32[]{:S(2)}) collective-permute-start(f32[8,16,128]{2,1,0:T(8,128)S(1)} %collective-permute-done.11), channel_id=1, source_target_pairs={{0,6},{1,3},{2,0},{3,5},{4,2},{5,7},{6,4},{7,1},{8,14},{9,11},{10,... | collective-permute-start | bytes 196616 | tf_op jit(solution)/shard_map/ppermute | solution.py:38
  97.8 1.3 collective-permute-start.27
  99.1 9.9 %collective-permute-start.29 = (bf16[4,2,256,128]{3,2,1,0:T(8,128)(2,1)S(1)}, bf16[4,2,256,128]{3,2,1,0:T(8,128)(2,1)S(1)}, u32[]{:S(2)}, u32[]{:S(2)}) collective-permute-start(bf16[4,2,256,128]{3,2,1,0:T(8,128)(2,1)S(1)} %pad_maximum_fusion.2.p0), channel_id=1, source_target_pairs={{0,64},{1,17},{2,66},{3,19},{4,68},{5,21},{6,70},{7,23},{8,72},{9,... | collective-permute-start | bytes 1572872 | tf_op jit(solution)/shard_map/ppermute | solution.py:42
  101.3 28.8 %copy-start.7 = (bf16[4,2,256,128]{3,2,1,0:T(8,128)(2,1)}, bf16[4,2,256,128]{3,2,1,0:T(8,128)(2,1)S(1)}, u32[]{:S(2)}) copy-start(bf16[4,2,256,128]{3,2,1,0:T(8,128)(2,1)S(1)} %collective-permute-done.28.p1) | copy-start | bytes 1572868
  101.3 13.4 %collective-permute-start.30 = (bf16[4,2,256,128]{3,2,1,0:T(8,128)(2,1)S(1)}, bf16[4,2,256,128]{3,2,1,0:T(8,128)(2,1)S(1)}, u32[]{:S(2)}, u32[]{:S(2)}) collective-permute-start(bf16[4,2,256,128]{3,2,1,0:T(8,128)(2,1)S(1)} %pad_maximum_fusion.2.p0), channel_id=1, source_target_pairs={{0,32},{1,9},{2,34},{3,11},{4,36},{5,13},{6,38},{7,15},{8,40},{9,1... | collective-permute-start | bytes 1572872 | tf_op jit(solution)/shard_map/ppermute | solution.py:42
  114.6 7.3 %copy-start.9 = (bf16[4,2,256,128]{3,2,1,0:T(8,128)(2,1)}, bf16[4,2,256,128]{3,2,1,0:T(8,128)(2,1)S(1)}, u32[]{:S(2)}) copy-start(bf16[4,2,256,128]{3,2,1,0:T(8,128)(2,1)S(1)} %collective-permute-done.30.p3) | copy-start | bytes 1572868
  121.9 8.2 %collective-permute-start.31 = (bf16[4,128,1024]{2,1,0:T(8,128)(2,1)}, bf16[4,128,1024]{2,1,0:T(8,128)(2,1)}, u32[]{:S(2)}, u32[]{:S(2)}) collective-permute-start(bf16[4,128,1024]{2,1,0:T(8,128)(2,1)} %collective-permute-done.25.far), channel_id=1, source_target_pairs={{0,1},{1,0},{2,3},{3,2},{4,5},{5,4},{6,7},{7,6},{8,9},{9,8},{10,11... | collective-permute-start | bytes 3145736 | tf_op jit(solution)/shard_map/ppermute | solution.py:38
  127.3 35.5 %collective-permute-start.23 = (bf16[4,128,1024]{2,1,0:T(8,128)(2,1)}, bf16[4,128,1024]{2,1,0:T(8,128)(2,1)}, u32[]{:S(2)}, u32[]{:S(2)}) collective-permute-start(bf16[4,128,1024]{2,1,0:T(8,128)(2,1)} %slice_bitcast_fusion), channel_id=1, source_target_pairs={{0,2},{1,7},{2,4},{3,1},{4,6},{5,3},{6,0},{7,5},{8,10},{9,15},{10,... | collective-permute-start | bytes 3145736 | tf_op jit(solution)/shard_map/ppermute | solution.py:38
  129.0 36.8 %collective-permute-start.22 = (bf16[2,4,128,1024]{3,2,1,0:T(8,128)(2,1)}, bf16[2,4,128,1024]{3,2,1,0:T(8,128)(2,1)S(1)}, u32[]{:S(2)}, u32[]{:S(2)}) collective-permute-start(bf16[2,4,128,1024]{3,2,1,0:T(8,128)(2,1)} %collective-permute-done.21.near), channel_id=1, source_target_pairs={{0,1},{1,0},{2,3},{3,2},{4,5},{5,4},{6,7},{7,6},{8,9},{9,8},{10,11... | collective-permute-start | bytes 6291464 | tf_op jit(solution)/shard_map/ppermute | solution.py:38
  162.8 3.1 %collective-permute-start.32 = (bf16[4,128,1024]{2,1,0:T(8,128)(2,1)}, bf16[4,128,1024]{2,1,0:T(8,128)(2,1)S(1)}, u32[]{:S(2)}, u32[]{:S(2)}) collective-permute-start(bf16[4,128,1024]{2,1,0:T(8,128)(2,1)} %collective-permute-done.23.far), channel_id=1, source_target_pairs={{0,1},{1,0},{2,3},{3,2},{4,5},{5,4},{6,7},{7,6},{8,9},{9,8},{10,11... | collective-permute-start | bytes 3145736 | tf_op jit(solution)/shard_map/ppermute | solution.py:38
  (7 other events, 11.9 us)
